TPU v7x, 256 devices: a whole 4x4x8 slice. The times are simulated.
256 devices in a mesh: gx: 16 (over z, core), gy: 8 (over x, y_hi), gz: 2 (over y_lo).
Axes of the slice: x: 4, y: 4 (y_hi: 2, y_lo: 2; y = y_hi * 2 + y_lo), z: 8, core: 2. Of those that a mesh axis runs over, the one named last changes fastest.
Arguments:
- body_force: bfloat16 [3, 256, 512, 256], P(None, 'gx', ('gy', 'gz')), may hold values from -6 to 6
- solid_mask: int32 [256, 512, 256], P('gx', ('gy', 'gz')), may hold values 0 or 1
- tracers: float32 [2, 256, 512, 256], P(None, 'gx', 'gy', 'gz'), may hold values from 0 to 1
- inlet_mask: int32 [2, 512, 256], P(None, 'gy', 'gz'), may hold values 0 or 1
Outputs:
- velocity: float32 [3, 256, 512, 256], P(None, 'gx', 'gy', 'gz')
- concentration: float32 [2, 256, 512, 256], P(None, 'gx', 'gy', 'gz')
All inputs are finite; a program needn't handle non-finite values. No bound on the sum of `solid_mask` or of `inlet_mask` on one device may be relied on, other than what follows from the above.
Results may differ from a plain program's by a relative error of at most 0.012.
Values may be sent and summed in bfloat16 or wider, within the bound.
A program may use at most 128 MiB of HBM per device.

v0:
```python
import math

import jax
import jax.numpy as jnp
from jax import lax
from jax.sharding import PartitionSpec as P

STEPS = 4


viscosity = 0.0625
screening = 0.25
time_step = 0.1


def with_halo(shard, sides, width):
    for axis, dim in sides:
        size, length = (lax.axis_size(axis), shard.shape[dim])
        up = [(i, (i + 1) % size) for i in range(size)]
        down = [(j, i) for i, j in up]
        last = lax.slice_in_dim(shard, length - width, length, axis=dim)
        first = lax.slice_in_dim(shard, 0, width, axis=dim)
        before = lax.ppermute(last, axis, up)
        after = lax.ppermute(first, axis, down)
        shard = jnp.concatenate([before, shard, after], axis=dim)
    return shard


def cos_sin(length):
    index = jnp.arange(length, dtype=jnp.int32)
    phase = (index[:, None] * index[None, :] % length).astype(jnp.float32) * (
        2.0 * math.pi / length
    )
    return (jnp.cos(phase).astype(jnp.bfloat16), jnp.sin(phase).astype(jnp.bfloat16))


def complex_table(length, forward):
    cos_t, sin_t = cos_sin(length)
    if forward:
        return jnp.stack([jnp.stack([cos_t, -sin_t], axis=1), jnp.stack([sin_t, cos_t], axis=1)])
    return jnp.stack([jnp.stack([cos_t, sin_t], axis=1), jnp.stack([-sin_t, cos_t], axis=1)])


def wavenumber(index, length):
    signed = jnp.where(index < length // 2, index, index - length)
    signed = jnp.where(index == length // 2, 0, signed)
    return signed.astype(jnp.float32) * (2.0 * math.pi / length)


def project(spectrum, waves, wave_sq, gain):
    inner = waves[0] * spectrum[0] + waves[1] * spectrum[1] + waves[2] * spectrum[2]
    along = jnp.where(wave_sq > 0, inner / jnp.where(wave_sq > 0, wave_sq, 1.0), 0.0)
    return jnp.stack(
        [
            gain * (spectrum[0] - waves[0] * along),
            gain * (spectrum[1] - waves[1] * along),
            gain * (spectrum[2] - waves[2] * along),
        ]
    )


def advance(padded, velocity):

    def shifted(dim, offset):
        cut = [slice(None), slice(2, -2), slice(2, -2), slice(2, -2)]
        cut[dim] = slice(2 + offset, padded.shape[dim] - 2 + offset)
        return padded[tuple(cut)]

    conc = shifted(1, 0)
    transport = jnp.zeros_like(conc)
    laplace = jnp.zeros_like(conc)
    for dim in (1, 2, 3):
        lower = shifted(dim, -1)
        lower_two = shifted(dim, -2)
        upper = shifted(dim, 1)
        upper_two = shifted(dim, 2)
        speed = velocity[dim - 1][None]
        behind = 1.5 * conc - 2.0 * lower + 0.5 * lower_two
        ahead = -1.5 * conc + 2.0 * upper - 0.5 * upper_two
        transport = transport + jnp.maximum(speed, 0.0) * behind + jnp.minimum(speed, 0.0) * ahead
        laplace = laplace + upper + lower - 2.0 * conc
    rates = jnp.array([0.05, 0.15], dtype=jnp.float32)[:, None, None, None]
    return conc - time_step * transport + time_step * rates * laplace


def per_device(body_force, solid_mask, tracers, inlet_mask):
    gx_count = lax.axis_size("gx")
    gy_count = lax.axis_size("gy")
    gz_count = lax.axis_size("gz")
    group_count = gy_count * gz_count
    comps, brick_x, pencil_y, z_length = body_force.shape
    x_length = brick_x * gx_count
    y_length = pencil_y * group_count
    kz_part = z_length // group_count
    ky_part = y_length // gx_count
    forcing = body_force * (1 - solid_mask).astype(jnp.bfloat16)[None]
    cos_z, sin_z = cos_sin(z_length)
    forward_z = jnp.stack([cos_z, -sin_z], axis=1)
    spectrum_z = jnp.einsum(
        "cxyn,nok->ocxyk", forcing, forward_z, preferred_element_type=jnp.float32
    ).astype(jnp.bfloat16)
    table_y = complex_table(y_length, True)
    spectrum_y = jnp.einsum(
        "icxnk,inoh->ockxh",
        lax.all_to_all(spectrum_z, ("gy", "gz"), split_axis=4, concat_axis=3, tiled=True),
        table_y,
        preferred_element_type=jnp.float32,
    ).astype(jnp.bfloat16)
    table_x = complex_table(x_length, True)
    spectrum_x = jnp.einsum(
        "ickns,inop->ocksp",
        lax.all_to_all(spectrum_y, "gx", split_axis=4, concat_axis=3, tiled=True),
        table_x,
        preferred_element_type=jnp.float32,
    )
    group_index = lax.axis_index("gy") * gz_count + lax.axis_index("gz")
    wave_x = wavenumber(jnp.arange(x_length, dtype=jnp.int32), x_length)[None, None, :]
    wave_y = wavenumber(
        lax.axis_index("gx") * ky_part + jnp.arange(ky_part, dtype=jnp.int32), y_length
    )[None, :, None]
    wave_z = wavenumber(group_index * kz_part + jnp.arange(kz_part, dtype=jnp.int32), z_length)[
        :, None, None
    ]
    wave_sq = wave_x * wave_x + wave_y * wave_y + wave_z * wave_z
    gain = 1.0 / ((viscosity * wave_sq + screening) * float(x_length * y_length * z_length))
    waves = (wave_x, wave_y, wave_z)
    green = jnp.stack(
        [project(spectrum_x[0], waves, wave_sq, gain), project(spectrum_x[1], waves, wave_sq, gain)]
    ).astype(jnp.bfloat16)
    inverse_x_table = complex_table(x_length, False)
    back_x = jnp.einsum(
        "icksp,ipon->ockns", green, inverse_x_table, preferred_element_type=jnp.float32
    ).astype(jnp.bfloat16)
    inverse_y_table = complex_table(y_length, False)
    rows_y = jnp.einsum(
        "ickxh,ihon->ockxn",
        lax.all_to_all(back_x, "gx", split_axis=3, concat_axis=4, tiled=True),
        inverse_y_table,
        preferred_element_type=jnp.float32,
    ).astype(jnp.bfloat16)
    inverse_z_table = jnp.stack([cos_z, -sin_z])
    pencil = jnp.einsum(
        "ickxy,ikn->cxyn",
        lax.all_to_all(rows_y, ("gy", "gz"), split_axis=4, concat_axis=2, tiled=True),
        inverse_z_table,
        preferred_element_type=jnp.float32,
    )
    velocity = lax.all_to_all(
        pencil.astype(jnp.bfloat16), "gz", split_axis=3, concat_axis=2, tiled=True
    ).astype(pencil.dtype)
    x_global = lax.axis_index("gx") * brick_x + jnp.arange(brick_x, dtype=jnp.int32)
    inlet = (x_global == 0)[None, :, None, None] & (inlet_mask == 1)[:, None, :, :]
    conc = jnp.where(inlet, jnp.float32(1.0), tracers)
    for step_index in range(STEPS):
        padded = with_halo(conc.astype(jnp.bfloat16), (("gx", 1), ("gy", 2), ("gz", 3)), 2).astype(
            conc.dtype
        )
        conc = advance(padded, velocity)
    return (velocity, conc)


def solution(mesh):
    in_specs = (
        P(None, "gx", ("gy", "gz"), None),
        P("gx", ("gy", "gz"), None),
        P(None, "gx", "gy", "gz"),
        P(None, "gy", "gz"),
    )
    out_specs = (P(None, "gx", "gy", "gz"), P(None, "gx", "gy", "gz"))
    return jax.shard_map(
        per_device, mesh=mesh, in_specs=in_specs, out_specs=out_specs, check_vma=False
    )
```

profile of v0, /device:TPU:24, one launch (start us, length us, event | category | flops | bytes accessed | tf_op | source)
XLA Modules:
  0.0 584.0 jit_solution(4888546621350347739)
XLA Ops:
  5.4 9.3 %copy.301 = bf16[2,3,16,32,256]{3,2,1,0,4:T(8,128)(2,1)} copy(bf16[2,3,16,32,256]{4,3,2,1,0:T(8,128)(2,1)S(1)} %fusion.110) | data formatting | bytes 3145728 | tf_op jit(solution)/shard_map/convert_element_type | solution.py:101
  14.7 9.3 %reshape.635 = bf16[16,2,24576]{2,1,0:T(2,128)(2,1)} reshape(bf16[256,2,3,16,32]{4,3,2,1,0:T(8,128)(2,1)} %bitcast.189) | data formatting | bytes 3145728
  24.0 7.8 %all-to-all-start = ((bf16[16,2,24576]{2,1,0:T(2,128)(2,1)}), bf16[16,2,24576]{2,1,0:T(2,128)(2,1)S(1)}, u32[]{:S(2)}, u32[]{:S(2)}) async-start(bf16[16,2,24576]{2,1,0:T(2,128)(2,1)} %reshape.635), calls=%async_computation | async-start | bytes 3145728 | tf_op jit(solution)/shard_map/all_to_all | solution.py:105
  31.8 4.0 fusion.157
  35.8 4.3 sine_convert_fusion
  42.3 9.9 %all-to-all-done = bf16[16,2,24576]{2,1,0:T(2,128)(2,1)S(1)} async-done(((bf16[16,2,24576]{2,1,0:T(2,128)(2,1)}), bf16[16,2,24576]{2,1,0:T(2,128)(2,1)S(1)}, u32[]{:S(2)}, u32[]{:S(2)}) %all-to-all-start) | async-done | bytes 1572896 | tf_op jit(solution)/shard_map/all_to_all | solution.py:105
  52.2 5.5 reshape.636
  57.7 9.5 %copy.303 = bf16[2,3,16,16,32,16]{4,3,5,0,2,1:T(8,128)(2,1)} copy(bf16[2,3,16,16,32,16]{4,2,1,0,5,3:T(8,128)(2,1)} %bitcast.187) | data formatting | bytes 3145728 | tf_op jit(solution)/shard_map/all_to_all | solution.py:105
  67.2 8.4 %reshape.620 = bf16[2,3,16,512,16,1]{3,4,0,2,1,5:T(8,128)(2,1)S(1)} reshape(bf16[2,3,16,16,32,16]{4,3,5,0,2,1:T(8,128)(2,1)} %copy.303) | data formatting | bytes 3145728 | tf_op jit(solution)/shard_map/all_to_all | solution.py:105
  75.6 3.3 fusion.111
  78.9 17.4 %copy.304 = bf16[2,3,16,16,512]{2,3,1,0,4:T(8,128)(2,1)} copy(bf16[2,3,16,16,512]{4,2,3,1,0:T(8,128)(2,1)S(1)} %fusion.111) | data formatting | bytes 3145728 | tf_op jit(solution)/shard_map/convert_element_type | solution.py:108
  96.3 17.7 %reshape.637 = bf16[16,2,24576]{2,1,0:T(2,128)(2,1)} reshape(bf16[512,2,3,16,16]{4,3,2,1,0:T(8,128)(2,1)} %bitcast.183) | data formatting | bytes 3145728
  114.0 8.7 %all-to-all-start.1 = ((bf16[16,2,24576]{2,1,0:T(2,128)(2,1)}), bf16[16,2,24576]{2,1,0:T(2,128)(2,1)S(1)}, u32[]{:S(2)}, u32[]{:S(2)}) async-start(bf16[16,2,24576]{2,1,0:T(2,128)(2,1)} %reshape.637), calls=%async_computation.1 | async-start | bytes 3145728 | tf_op jit(solution)/shard_map/all_to_all | solution.py:112
  124.0 36.5 %all-to-all-done.1 = bf16[16,2,24576]{2,1,0:T(2,128)(2,1)S(1)} async-done(((bf16[16,2,24576]{2,1,0:T(2,128)(2,1)}), bf16[16,2,24576]{2,1,0:T(2,128)(2,1)S(1)}, u32[]{:S(2)}, u32[]{:S(2)}) %all-to-all-start.1) | async-done | bytes 1572896 | tf_op jit(solution)/shard_map/all_to_all | solution.py:112
  160.6 12.2 %reshape.638 = bf16[512,2,3,16,16]{4,3,2,1,0:T(8,128)(2,1)} reshape(bf16[16,2,24576]{2,1,0:T(2,128)(2,1)S(1)} %all-to-all-done.1) | data formatting | bytes 3145728
  172.7 18.1 %copy.305 = bf16[2,3,16,16,16,32]{5,3,4,2,1,0:T(8,128)(2,1)} copy(bf16[2,3,16,16,16,32]{2,3,1,0,5,4:T(8,128)(2,1)} %bitcast.184) | data formatting | bytes 3145728 | tf_op jit(solution)/shard_map/all_to_all | solution.py:112
  190.8 4.6 fusion.100
  198.1 9.3 %copy.310 = bf16[2,3,16,256,32]{4,2,1,0,3:T(8,128)(2,1)} copy(bf16[2,3,16,256,32]{3,4,2,1,0:T(8,128)(2,1)S(1)} %fusion.114) | data formatting | bytes 3145728 | tf_op jit(solution)/shard_map/convert_element_type | solution.py:133
  207.3 8.4 %reshape.639 = bf16[16,2,24576]{2,1,0:T(2,128)(2,1)S(1)} reshape(bf16[256,2,3,16,32]{4,3,2,1,0:T(8,128)(2,1)} %bitcast.190) | data formatting | bytes 3145728
  215.8 43.4 %all_to_all.81 = bf16[16,2,24576]{2,1,0:T(2,128)(2,1)S(1)} all-to-all(bf16[16,2,24576]{2,1,0:T(2,128)(2,1)S(1)} %reshape.639), channel_id=1, replica_groups=mesh['gx'=16,'gy'=8,'gz'=2] {'gx'}, dimensions={0} | all-to-all | bytes 3145728 | tf_op jit(solution)/shard_map/all_to_all | solution.py:137
  259.1 5.5 reshape.640
  264.6 9.5 %copy.312 = bf16[2,3,16,16,16,32]{5,4,3,0,2,1:T(8,128)(2,1)} copy(bf16[2,3,16,16,16,32]{5,2,1,0,3,4:T(8,128)(2,1)} %bitcast.188) | data formatting | bytes 3145728 | tf_op jit(solution)/shard_map/all_to_all | solution.py:137
  274.1 8.4 %reshape.629 = bf16[2,3,16,16,512,1]{4,3,0,2,1,5:T(8,128)(2,1)S(1)} reshape(bf16[2,3,16,16,16,32]{5,4,3,0,2,1:T(8,128)(2,1)} %copy.312) | data formatting | bytes 3145728 | tf_op jit(solution)/shard_map/all_to_all | solution.py:137
  282.5 3.3 fusion.107
  285.8 17.4 %copy.314 = bf16[2,3,16,16,512]{3,2,1,0,4:T(8,128)(2,1)} copy(bf16[2,3,16,16,512]{4,3,2,1,0:T(8,128)(2,1)S(1)} %fusion.107) | data formatting | bytes 3145728 | tf_op jit(solution)/shard_map/convert_element_type | solution.py:140
  303.3 17.7 %reshape.641 = bf16[16,2,24576]{2,1,0:T(2,128)(2,1)} reshape(bf16[512,2,3,16,16]{4,3,2,1,0:T(8,128)(2,1)} %bitcast.185) | data formatting | bytes 3145728
  320.9 7.8 %all-to-all-start.3 = ((bf16[16,2,24576]{2,1,0:T(2,128)(2,1)}), bf16[16,2,24576]{2,1,0:T(2,128)(2,1)S(1)}, u32[]{:S(2)}, u32[]{:S(2)}) async-start(bf16[16,2,24576]{2,1,0:T(2,128)(2,1)} %reshape.641), calls=%async_computation.3 | async-start | bytes 3145728 | tf_op jit(solution)/shard_map/all_to_all | solution.py:144
  334.9 17.0 %all-to-all-done.3 = bf16[16,2,24576]{2,1,0:T(2,128)(2,1)S(1)} async-done(((bf16[16,2,24576]{2,1,0:T(2,128)(2,1)}), bf16[16,2,24576]{2,1,0:T(2,128)(2,1)S(1)}, u32[]{:S(2)}, u32[]{:S(2)}) %all-to-all-start.3) | async-done | bytes 1572896 | tf_op jit(solution)/shard_map/all_to_all | solution.py:144
  351.9 12.2 %reshape.642 = bf16[512,2,3,16,16]{4,3,2,1,0:T(8,128)(2,1)} reshape(bf16[16,2,24576]{2,1,0:T(2,128)(2,1)S(1)} %all-to-all-done.3) | data formatting | bytes 3145728
  364.0 14.8 %copy.315 = bf16[2,3,16,16,16,32]{5,3,2,4,1,0:T(8,128)(2,1)} copy(bf16[2,3,16,16,16,32]{3,2,1,0,5,4:T(8,128)(2,1)} %bitcast.186) | data formatting | bytes 3145728 | tf_op jit(solution)/shard_map/all_to_all | solution.py:144
  378.8 5.5 bitcast_convert_fusion.3
  384.4 3.8 copy.317
  388.2 3.8 reshape.643
  392.1 5.6 all-to-all-start.4
  403.9 6.3 %collective-permute-done.2 = bf16[2,20,2,128]{3,1,2,0:T(8,128)(2,1)S(1)} collective-permute-done((bf16[2,20,2,128]{3,1,2,0:T(8,128)(2,1)S(1)}, bf16[2,20,2,128]{3,1,2,0:T(8,128)(2,1)S(1)}, u32[]{:S(2)}, u32[]{:S(2)}) %collective-permute-start.2) | collective-permute-done | bytes 20512 | tf_op jit(solution)/shard_map/ppermute | solution.py:23
  417.5 3.3 maximum_convert_fusion
  420.8 3.9 reshape.644
  424.7 4.8 copy.318
  448.4 8.6 %fusion.72 = bf16[2,16,64,128]{2,1,3,0:T(8,128)(2,1)S(1)} fusion(f32[2,20,68,132]{2,1,3,0:T(8,128)S(1)} %maximum_convert_fusion, f32[2]{0:T(128)S(1)} %copy-done.20, f32[16,64,128]{1,0,2:T(8,128)} %copy.330, f32[16,64,128]{1,0,2:T(8,128)} %copy.329, f32[16,64,128]{1,0,2:T(8,128)} %copy.328, f32[16,64,128]{1,0,2:T(8,128)} %copy.327, ...), kind=kLoop, calls=%fused_computation.94 | loop fusion | flops 13369344 | bytes 17301512 | tf_op jit(solution)/shard_map/convert_element_type | solution.py:155
  457.2 2.9 collective-permute-start.7
  469.1 3.5 collective-permute-start.9
  483.9 3.5 maximum_convert_fusion.1
  487.4 9.2 %fusion.51 = bf16[2,16,64,128]{2,1,3,0:T(8,128)(2,1)} fusion(f32[2,20,68,132]{2,1,3,0:T(8,128)S(1)} %maximum_convert_fusion.1, f32[2]{0:T(128)S(1)} %copy-done.20, f32[16,64,128]{1,0,2:T(8,128)} %copy.330, f32[16,64,128]{1,0,2:T(8,128)} %copy.329, f32[16,64,128]{1,0,2:T(8,128)} %copy.328, f32[16,64,128]{1,0,2:T(8,128)} %copy.327, f32[16,64,128]{1,0,2:T(8,128)} %copy.326, ...), kind=kLoop, calls=%fused_computation.67 | loop fusion | flops 13369344 | bytes 17301512 | tf_op jit(solution)/shard_map/convert_element_type | solution.py:155
  516.3 3.5 collective-permute-done.15
  529.4 9.2 %fusion.30 = bf16[2,16,64,128]{2,1,3,0:T(8,128)(2,1)} fusion(f32[2,20,68,132]{2,1,3,0:T(8,128)S(1)} %maximum_convert_fusion.2, f32[2]{0:T(128)S(1)} %copy-done.20, f32[16,64,128]{1,0,2:T(8,128)} %copy.330, f32[16,64,128]{1,0,2:T(8,128)} %copy.329, f32[16,64,128]{1,0,2:T(8,128)} %copy.328, f32[16,64,128]{1,0,2:T(8,128)} %copy.327, f32[16,64,128]{1,0,2:T(8,128)} %copy.326, ...), kind=kLoop, calls=%fused_computation.40 | loop fusion | flops 13369344 | bytes 17301512 | tf_op jit(solution)/shard_map/convert_element_type | solution.py:155
  558.3 3.5 collective-permute-done.21
  571.1 9.4 %fusion.9 = f32[2,16,64,128]{2,1,3,0:T(8,128)} fusion(f32[2,20,68,132]{2,1,3,0:T(8,128)S(1)} %maximum_convert_fusion.3, f32[2]{0:T(128)S(1)} %copy-done.20, f32[16,64,128]{1,0,2:T(8,128)} %copy.330, f32[16,64,128]{1,0,2:T(8,128)} %copy.329, f32[16,64,128]{1,0,2:T(8,128)} %copy.328, f32[16,64,128]{1,0,2:T(8,128)} %copy.327, f32[16,64,128]{1,0,2:T(8,128)} %copy.326, ...), kind=kLoop, calls=%fused_computation.13 | loop fusion | flops 13107200 | bytes 17825800 | tf_op jit(solution)/shard_map/add | solution.py:83
  580.5 3.3 copy.343
  (152 shorter events, 127.7 us)
Async XLA Ops:
  24.0 28.2 %all-to-all-start = ((bf16[16,2,24576]{2,1,0:T(2,128)(2,1)}), bf16[16,2,24576]{2,1,0:T(2,128)(2,1)S(1)}, u32[]{:S(2)}, u32[]{:S(2)}) async-start(bf16[16,2,24576]{2,1,0:T(2,128)(2,1)} %reshape.635), calls=%async_computation | async-start | bytes 3145728 | tf_op jit(solution)/shard_map/all_to_all | solution.py:105
  114.0 46.6 %all-to-all-start.1 = ((bf16[16,2,24576]{2,1,0:T(2,128)(2,1)}), bf16[16,2,24576]{2,1,0:T(2,128)(2,1)S(1)}, u32[]{:S(2)}, u32[]{:S(2)}) async-start(bf16[16,2,24576]{2,1,0:T(2,128)(2,1)} %reshape.637), calls=%async_computation.1 | async-start | bytes 3145728 | tf_op jit(solution)/shard_map/all_to_all | solution.py:112
  320.9 7.8 %copy-start.19 = (s32[2,64,128]{2,1,0:T(8,128)S(1)}, s32[2,64,128]{2,1,0:T(8,128)}, u32[]{:S(2)}) copy-start(s32[2,64,128]{2,1,0:T(8,128)} %param.11) | copy-start | bytes 196612
  320.9 7.9 %copy-start.18 = (f32[2,16,64,128]{3,2,1,0:T(8,128)S(1)}, f32[2,16,64,128]{3,2,1,0:T(8,128)}, u32[]{:S(2)}) copy-start(f32[2,16,64,128]{3,2,1,0:T(8,128)} %param.10) | copy-start | bytes 3145732
  320.9 31.0 %all-to-all-start.3 = ((bf16[16,2,24576]{2,1,0:T(2,128)(2,1)}), bf16[16,2,24576]{2,1,0:T(2,128)(2,1)S(1)}, u32[]{:S(2)}, u32[]{:S(2)}) async-start(bf16[16,2,24576]{2,1,0:T(2,128)(2,1)} %reshape.641), calls=%async_computation.3 | async-start | bytes 3145728 | tf_op jit(solution)/shard_map/all_to_all | solution.py:144
  329.0 4.9 collective-permute-start
  330.2 3.8 collective-permute-start.1
  392.1 10.2 %copy-start.17 = (bf16[2,20,64,128]{3,2,1,0:T(8,128)(2,1)S(1)}, bf16[2,20,64,128]{3,2,1,0:T(8,128)(2,1)}, u32[]{:S(2)}) copy-start(bf16[2,20,64,128]{3,2,1,0:T(8,128)(2,1)} %pad_maximum_fusion.8) | copy-start | bytes 1966084
  392.1 28.8 %all-to-all-start.4 = ((bf16[2,2,98304]{2,1,0:T(2,128)(2,1)}), bf16[2,2,98304]{2,1,0:T(2,128)(2,1)}, u32[]{:S(2)}, u32[]{:S(2)}) async-start(bf16[2,2,98304]{2,1,0:T(2,128)(2,1)} %reshape.643), calls=%async_computation.4 | async-start | bytes 1572864 | tf_op jit(solution)/shard_map/all_to_all | solution.py:148
  398.6 11.6 %collective-permute-start.2 = (bf16[2,20,2,128]{3,1,2,0:T(8,128)(2,1)S(1)}, bf16[2,20,2,128]{3,1,2,0:T(8,128)(2,1)S(1)}, u32[]{:S(2)}, u32[]{:S(2)}) collective-permute-start(bf16[2,20,2,128]{3,1,2,0:T(8,128)(2,1)S(1)} %copy.366), channel_id=1, source_target_pairs={{0,2},{2,4},{4,6},{6,8},{8,10},{10,12},{12,14},{14,0},{1,3},{3,5},... | collective-permute-start | bytes 61448 | tf_op jit(solution)/shard_map/ppermute | solution.py:23
  399.9 11.3 %collective-permute-start.3 = (bf16[2,20,2,128]{3,1,2,0:T(8,128)(2,1)S(1)}, bf16[2,20,2,128]{3,1,2,0:T(8,128)(2,1)S(1)}, u32[]{:S(2)}, u32[]{:S(2)}) collective-permute-start(bf16[2,20,2,128]{3,1,2,0:T(8,128)(2,1)S(1)} %copy.367), channel_id=1, source_target_pairs={{2,0},{4,2},{6,4},{8,6},{10,8},{12,10},{14,12},{0,14},{3,1},{5,3},... | collective-permute-start | bytes 61448 | tf_op jit(solution)/shard_map/ppermute | solution.py:24
  411.2 2.1 copy-start.14
  412.2 5.3 copy-start.16
  413.4 3.8 collective-permute-start.4
  413.4 4.1 collective-permute-start.5
  441.1 7.3 %copy-start.20 = (f32[2]{0:T(128)S(1)}, f32[2]{0:T(128)}, u32[]{:S(2)}) copy-start(f32[2]{0:T(128)} %constant.110) | copy-start | bytes 28
  457.0 8.6 %copy-start.1 = (bf16[2,16,64,128]{2,1,3,0:T(8,128)(2,1)}, bf16[2,16,64,128]{2,1,3,0:T(8,128)(2,1)S(1)}, u32[]{:S(2)}) copy-start(bf16[2,16,64,128]{2,1,3,0:T(8,128)(2,1)S(1)} %fusion.72) | copy-start | bytes 1572868
  457.2 5.6 collective-permute-start.6
  457.2 5.6 collective-permute-start.7
  467.8 5.4 collective-permute-start.8
  468.1 9.2 %copy-start.2 = (bf16[2,16,64,128]{2,1,3,0:T(8,128)(2,1)S(1)}, bf16[2,16,64,128]{2,1,3,0:T(8,128)(2,1)}, u32[]{:S(2)}) copy-start(bf16[2,16,64,128]{2,1,3,0:T(8,128)(2,1)} %copy-done.1) | copy-start | bytes 1572868
  469.1 6.5 %collective-permute-start.9 = (bf16[2,20,2,128]{3,1,2,0:T(8,128)(2,1)S(1)}, bf16[2,20,2,128]{3,1,2,0:T(8,128)(2,1)S(1)}, u32[]{:S(2)}, u32[]{:S(2)}) collective-permute-start(bf16[2,20,2,128]{3,1,2,0:T(8,128)(2,1)S(1)} %copy.332), channel_id=1, source_target_pairs={{2,0},{4,2},{6,4},{8,6},{10,8},{12,10},{14,12},{0,14},{3,1},{5,3},... | collective-permute-start | bytes 61448 | tf_op jit(solution)/shard_map/ppermute | solution.py:24
  474.1 4.2 copy-start.8
  477.3 6.6 %copy-start.3 = (bf16[2,16,64,128]{2,1,3,0:T(8,128)(2,1)S(1)}, bf16[2,16,64,128]{2,1,3,0:T(8,128)(2,1)}, u32[]{:S(2)}) copy-start(bf16[2,16,64,128]{2,1,3,0:T(8,128)(2,1)} %copy-done.1) | copy-start | bytes 1572868
  477.3 6.6 %copy-start.11 = (bf16[2,20,2,128]{2,1,3,0:T(8,128)(2,1)S(1)}, bf16[2,20,2,128]{2,1,3,0:T(8,128)(2,1)}, u32[]{:S(2)}) copy-start(bf16[2,20,2,128]{2,1,3,0:T(8,128)(2,1)} %copy.334) | copy-start | bytes 61444
  478.4 3.9 collective-permute-start.10
  480.1 7.3 %copy-start = (f32[16,64,128]{1,0,2:T(8,128)S(1)}, f32[16,64,128]{1,0,2:T(8,128)}, u32[]{:S(2)}) copy-start(f32[16,64,128]{1,0,2:T(8,128)} %copy.325) | copy-start | bytes 1572868
  480.1 3.8 collective-permute-start.11
  498.1 5.6 collective-permute-start.12
  498.1 5.6 collective-permute-start.13
  508.7 5.9 %collective-permute-start.14 = (bf16[2,20,2,128]{3,1,2,0:T(8,128)(2,1)S(1)}, bf16[2,20,2,128]{3,1,2,0:T(8,128)(2,1)S(1)}, u32[]{:S(2)}, u32[]{:S(2)}) collective-permute-start(bf16[2,20,2,128]{3,1,2,0:T(8,128)(2,1)S(1)} %copy.335), channel_id=1, source_target_pairs={{0,2},{2,4},{4,6},{6,8},{8,10},{10,12},{12,14},{14,0},{1,3},{3,5},... | collective-permute-start | bytes 61448 | tf_op jit(solution)/shard_map/ppermute | solution.py:23
  511.2 10.3 %copy-start.4 = (bf16[2,16,64,128]{2,1,3,0:T(8,128)(2,1)S(1)}, bf16[2,16,64,128]{2,1,3,0:T(8,128)(2,1)}, u32[]{:S(2)}) copy-start(bf16[2,16,64,128]{2,1,3,0:T(8,128)(2,1)} %fusion.51) | copy-start | bytes 1572868
  513.5 6.3 %collective-permute-start.15 = (bf16[2,20,2,128]{3,1,2,0:T(8,128)(2,1)S(1)}, bf16[2,20,2,128]{3,1,2,0:T(8,128)(2,1)S(1)}, u32[]{:S(2)}, u32[]{:S(2)}) collective-permute-start(bf16[2,20,2,128]{3,1,2,0:T(8,128)(2,1)S(1)} %copy.336), channel_id=1, source_target_pairs={{2,0},{4,2},{6,4},{8,6},{10,8},{12,10},{14,12},{0,14},{3,1},{5,3},... | collective-permute-start | bytes 61448 | tf_op jit(solution)/shard_map/ppermute | solution.py:24
  521.5 5.5 copy-start.5
  521.5 5.5 copy-start.9
  521.5 5.5 copy-start.12
  522.6 3.9 collective-permute-start.16
  522.7 4.3 collective-permute-start.17
  540.0 5.6 collective-permute-start.18
  540.0 5.6 collective-permute-start.19
  550.6 5.9 %collective-permute-start.20 = (bf16[2,20,2,128]{3,1,2,0:T(8,128)(2,1)S(1)}, bf16[2,20,2,128]{3,1,2,0:T(8,128)(2,1)S(1)}, u32[]{:S(2)}, u32[]{:S(2)}) collective-permute-start(bf16[2,20,2,128]{3,1,2,0:T(8,128)(2,1)S(1)} %copy.339), channel_id=1, source_target_pairs={{0,2},{2,4},{4,6},{6,8},{8,10},{10,12},{12,14},{14,0},{1,3},{3,5},... | collective-permute-start | bytes 61448 | tf_op jit(solution)/shard_map/ppermute | solution.py:23
  553.2 10.3 %copy-start.6 = (bf16[2,16,64,128]{2,1,3,0:T(8,128)(2,1)S(1)}, bf16[2,16,64,128]{2,1,3,0:T(8,128)(2,1)}, u32[]{:S(2)}) copy-start(bf16[2,16,64,128]{2,1,3,0:T(8,128)(2,1)} %fusion.30) | copy-start | bytes 1572868
  555.5 6.3 %collective-permute-start.21 = (bf16[2,20,2,128]{3,1,2,0:T(8,128)(2,1)S(1)}, bf16[2,20,2,128]{3,1,2,0:T(8,128)(2,1)S(1)}, u32[]{:S(2)}, u32[]{:S(2)}) collective-permute-start(bf16[2,20,2,128]{3,1,2,0:T(8,128)(2,1)S(1)} %copy.340), channel_id=1, source_target_pairs={{2,0},{4,2},{6,4},{8,6},{10,8},{12,10},{14,12},{0,14},{3,1},{5,3},... | collective-permute-start | bytes 61448 | tf_op jit(solution)/shard_map/ppermute | solution.py:24
  563.5 5.3 copy-start.7
  563.5 5.3 copy-start.10
  563.5 5.3 copy-start.13
  564.6 3.9 collective-permute-start.22
  564.7 4.1 collective-permute-start.23
  (1 other events, 1.2 us)
where the time goes:
time: 595 us; the launch traced here: 584 us
  local copies, waits for them, and re-layouts  277 us (47%)
  waiting for transfers between devices  96 us (16%)
  other arithmetic  80.8 us (14%)
  starting transfers between devices  65.6 us (11%)
  blocking collectives  43.4 us (7%)
  matrix products  19.5 us (3%)
    unnamed x55, local copies, waits for them, and re-layouts  99.6 us
    all_to_all x1, blocking collectives, per_device(): lax.all_to_all(back_x, 'gx', split_axis=3, concat_axis=4, tiled=True)  43.4 us
    all_to_all x1, waiting for transfers between devices, per_device(): lax.all_to_all(spectrum_y, 'gx', split_axis=4, concat_axis=3, tiled=True)  36.5 us
    convert_element_type x4, other arithmetic, per_device(): conc.astype(jnp.bfloat16)  27.3 us
    ppermute x12, starting transfers between devices, with_halo(): after = lax.ppermute(first, axis, down)  25.8 us
    ppermute x12, waiting for transfers between devices, with_halo(): before = lax.ppermute(last, axis, up)  21.3 us
    all_to_all x1, local copies, waits for them, and re-layouts, per_device(): lax.all_to_all(spectrum_y, 'gx', split_axis=4, concat_axis=3, tiled=True)  18.1 us
    all_to_all x2, local copies, waits for them, and re-layouts, per_device(): lax.all_to_all(back_x, 'gx', split_axis=3, concat_axis=4, tiled=True)  17.9 us
  transfers between devices with their start and end apart: 28, of which 19 were waited for; matrix products, arithmetic and copies ran while one was open for 6% of the time, Pallas kernels for 0%

commit v1 on v0

v1 whole, which is shorter than its diff:
```python
import functools
import math

import jax
import jax.numpy as jnp
import numpy as np
from jax import lax
from jax.experimental import pallas as pl
from jax.experimental.pallas import tpu as pltpu
from jax.sharding import PartitionSpec as P

STEPS = 4
VISCOSITY = 0.0625
SCREENING = 0.25
TIME_STEP = 0.1
RATES = (0.05, 0.15)

MESH = pl.DeviceIdType.MESH
BF16 = jnp.bfloat16
F32 = jnp.float32
GRID_X, GRID_Y, GRID_Z = 256, 512, 256
KZ = GRID_Z // 2
VMEM_LIMIT = 60 * 1024 * 1024


def cos_sin(length):
    index = np.arange(length)
    phase = (index[:, None] * index[None, :] % length) * (2.0 * math.pi / length)
    return np.cos(phase), np.sin(phase)


def z_tables():
    cos_t, sin_t = cos_sin(GRID_Z)
    forward = np.concatenate([cos_t[:, :KZ], -sin_t[:, :KZ]], axis=1)
    forward[:, KZ] = cos_t[:, KZ]
    inverse = np.concatenate([2.0 * cos_t[:KZ], -2.0 * sin_t[:KZ]], axis=0)
    inverse[0] = cos_t[0]
    inverse[KZ] = cos_t[KZ]
    return forward.astype(jnp.bfloat16), inverse.astype(jnp.bfloat16)


def y_table():
    cos_t, sin_t = cos_sin(GRID_Y)
    return np.concatenate([cos_t, sin_t], axis=1).astype(jnp.bfloat16)


def x_tables():
    cos_t, sin_t = cos_sin(GRID_X)
    order = np.arange(GRID_X).reshape(2, 8, 16).transpose(0, 2, 1).reshape(-1)
    cos_p, sin_p = cos_t[order], sin_t[order]
    forward = np.block([[cos_p, -sin_p], [sin_p, cos_p]])
    inverse = np.block([[cos_p.T, sin_p.T], [-sin_p.T, cos_p.T]])
    return forward.astype(jnp.bfloat16), inverse.astype(jnp.bfloat16)


def swap_index_and_lanes(parts, unit):
    lane = lax.broadcasted_iota(jnp.int32, parts[0].shape, 1)
    step = 1
    while step < len(parts):
        shift = unit * step
        upper = (lane & shift) != 0
        after = list(parts)
        for a in range(len(parts)):
            if a & step:
                continue
            low, high = parts[a], parts[a | step]
            after[a] = jnp.where(upper, pltpu.roll(high, shift, 1), low)
            after[a | step] = jnp.where(upper, high, pltpu.roll(low, 128 - shift, 1))
        parts = after
        step *= 2
    return parts


def signed_wave(index, length):
    signed = jnp.where(index < length // 2, index, index - length)
    signed = jnp.where(index == length // 2, 0, signed)
    return signed.astype(F32) * (2.0 * math.pi / length)


def spectral_kernel(
    force_hbm, mask_hbm, fz_hbm, iz_hbm, ty_hbm, fx_hbm, ix_hbm, vel_ref,
    force, mask, fz, iz, ty, fx, ix, zbuf, rhs, xin, spec, green, zin,
    send1, recv1, send2, recv2, send3, recv3, send4, recv4, sendv, recvv,
    load_sem, send_sem, recv_sem, vsend_sem, vrecv_sem,
):
    gx, gy, gz = lax.axis_index("gx"), lax.axis_index("gy"), lax.axis_index("gz")
    group = gy * 2 + gz

    def in_plane(to):
        return (gx, to // 2, to % 2)

    def in_column(to):
        return (to, gy, gz)

    loads = [
        pltpu.make_async_copy(src, dst, load_sem.at[n])
        for n, (src, dst) in enumerate(
            [(fz_hbm, fz), (mask_hbm, mask), (force_hbm, force), (ty_hbm, ty), (fx_hbm, fx), (ix_hbm, ix), (iz_hbm, iz)]
        )
    ]
    for load in loads:
        load.start()

    barrier = pltpu.get_barrier_semaphore()

    def greet(k, carry):
        pl.semaphore_signal(barrier, inc=1, device_id=in_plane((group + k) % 16), device_id_type=MESH)
        pl.semaphore_signal(barrier, inc=1, device_id=in_column((gx + k) % 16), device_id_type=MESH)
        return carry

    lax.fori_loop(1, 16, greet, 0)

    def exchange(stage, c, send, recv, me, place):
        def one(k, carry):
            to = (me + k) % 16
            pltpu.make_async_remote_copy(
                src_ref=send.at[c, to], dst_ref=recv.at[c, me],
                send_sem=send_sem.at[stage, c], recv_sem=recv_sem.at[stage, c],
                device_id=place(to), device_id_type=MESH,
            ).start()
            return carry

        lax.fori_loop(1, 16, one, 0)
        pltpu.make_async_copy(send.at[c, me], recv.at[c, me], recv_sem.at[stage, c]).start()

    def arrived(stage, c, recv):
        pltpu.make_async_copy(recv.at[c], recv.at[c], recv_sem.at[stage, c]).wait()

    def sent(stage, c, send):
        pltpu.make_async_copy(send.at[c, pl.ds(0, 15)], send.at[c, pl.ds(0, 15)], send_sem.at[stage, c]).wait()

    for load in loads[:3]:
        load.wait()

    def forward_z(c, carry):
        for h in range(2):
            rows = slice(8 * h, 8 * h + 8)
            kept = jnp.where(mask[rows] == 0, force[c, rows].astype(F32), 0.0).astype(BF16)
            out = jnp.dot(kept.reshape(256, 256), fz[...], preferred_element_type=F32)
            zbuf[rows] = out.reshape(8, 32, 256)
        for ri in range(2):
            for y in (0, 16):
                parts = [zbuf[x, y:y + 16, 128 * ri:128 * ri + 128] for x in range(16)]
                parts = swap_index_and_lanes(parts, 8)
                for to in range(16):
                    send1[c, to, ri, y:y + 16, :] = parts[to].astype(BF16)

        @pl.when(c == 0)
        def _():
            pl.semaphore_wait(barrier, 30)

        exchange(0, c, send1, recv1, group, in_plane)
        return carry

    lax.fori_loop(0, 3, forward_z, 0)

    def y_transform(recv, send, c, forward):
        re = recv[c, :, 0].reshape(512, 128)
        im = recv[c, :, 1].reshape(512, 128)
        rhs[0:512, 0:128] = re
        rhs[0:512, 128:256] = im
        rhs[512:1024, 0:128] = im if forward else -im
        rhs[512:1024, 128:256] = -re if forward else re
        for h in range(2):
            out = jnp.dot(ty[256 * h:256 * h + 256, :], rhs[...], preferred_element_type=F32)
            out = out.astype(BF16).reshape(8, 32, 256)
            send[c, 8 * h:8 * h + 8, 0] = out[:, :, 0:128]
            send[c, 8 * h:8 * h + 8, 1] = out[:, :, 128:256]

    loads[3].wait()

    def forward_y(c, carry):
        arrived(0, c, recv1)
        y_transform(recv1, send2, c, True)
        exchange(1, c, send2, recv2, gx, in_column)
        return carry

    lax.fori_loop(0, 3, forward_y, 0)

    loads[4].wait()

    def forward_x(c, carry):
        arrived(1, c, recv2)
        for ri in range(2):
            for hi in range(2):
                for ky in (0, 16):
                    parts = [recv2[c, 8 * hi + i, ri, ky:ky + 16, :].astype(F32) for i in range(8)]
                    parts = swap_index_and_lanes(parts, 1)
                    lanes = slice(256 * ri + 128 * hi, 256 * ri + 128 * hi + 128)
                    for k in range(8):
                        xin[k, ky:ky + 16, lanes] = parts[k].astype(BF16)
        spec[c] = jnp.dot(xin[...].reshape(256, 512), fx[...], preferred_element_type=F32)
        return carry

    lax.fori_loop(0, 3, forward_x, 0)

    wave_x = signed_wave(lax.broadcasted_iota(jnp.int32, (16, GRID_X), 1), GRID_X)
    row = lax.broadcasted_iota(jnp.int32, (16, GRID_X), 0)

    def project(b, carry):
        at = pl.ds(pl.multiple_of(b * 16, 16), 16)
        wave_y = signed_wave(gx * 32 + (b % 2) * 16 + row, GRID_Y)
        wave_z = signed_wave(group * 8 + b // 2 + jnp.zeros_like(row), GRID_Z)
        wave_sq = wave_x * wave_x + wave_y * wave_y + wave_z * wave_z
        gain = 1.0 / ((VISCOSITY * wave_sq + SCREENING) * float(GRID_X * GRID_Y * GRID_Z))
        inverse_sq = jnp.where(wave_sq > 0, 1.0 / jnp.where(wave_sq > 0, wave_sq, 1.0), 0.0)
        waves = (wave_x, wave_y, wave_z)
        for lanes in (slice(0, 256), slice(256, 512)):
            parts = [spec[c, at, lanes] for c in range(3)]
            inner = waves[0] * parts[0] + waves[1] * parts[1] + waves[2] * parts[2]
            along = inner * inverse_sq
            for c in range(3):
                green[c, at, lanes] = (gain * (parts[c] - waves[c] * along)).astype(BF16)
        return carry

    lax.fori_loop(0, 16, project, 0)

    loads[5].wait()

    def inverse_x(c, carry):
        spec[c] = jnp.dot(green[c], ix[...], preferred_element_type=F32)
        for ro in range(2):
            for hi in range(2):
                for ky in (0, 16):
                    first = 256 * ro + 128 * hi
                    parts = [spec[c, 32 * k + ky:32 * k + ky + 16, first:first + 128] for k in range(8)]
                    parts = swap_index_and_lanes(parts, 1)
                    for i in range(8):
                        send3[c, 8 * hi + i, ro, ky:ky + 16, :] = parts[i].astype(BF16)
        exchange(2, c, send3, recv3, gx, in_column)
        return carry

    lax.fori_loop(0, 3, inverse_x, 0)

    def inverse_y(c, carry):
        arrived(2, c, recv3)
        y_transform(recv3, send4, c, False)
        exchange(3, c, send4, recv4, group, in_plane)
        return carry

    lax.fori_loop(0, 3, inverse_y, 0)

    loads[6].wait()
    own = pl.multiple_of(gz * 32, 32)
    other = pl.multiple_of((1 - gz) * 32, 32)

    def to_partner(c):
        return pltpu.make_async_remote_copy(
            src_ref=sendv.at[c], dst_ref=recvv.at[c], send_sem=vsend_sem.at[c], recv_sem=vrecv_sem.at[c],
            device_id=(gx, gy, 1 - gz), device_id_type=MESH,
        )

    def inverse_z(c, carry):
        arrived(3, c, recv4)
        for ro in range(2):
            for y in (0, 16):
                parts = [recv4[c, s, ro, y:y + 16, :].astype(F32) for s in range(16)]
                parts = swap_index_and_lanes(parts, 8)
                for x in range(16):
                    zin[x, y:y + 16, 128 * ro:128 * ro + 128] = parts[x].astype(BF16)
        for h in range(2):
            rows = slice(8 * h, 8 * h + 8)
            out = jnp.dot(zin[rows].reshape(256, 256), iz[...], preferred_element_type=F32)
            zbuf[rows] = out.reshape(8, 32, 256)
        mine = pl.ds(pl.multiple_of(gz * 128, 128), 128)
        theirs = pl.ds(pl.multiple_of((1 - gz) * 128, 128), 128)
        sendv[c] = zbuf[:, :, theirs].astype(BF16)
        to_partner(c).start()
        vel_ref[c, :, pl.ds(own, 32), :] = zbuf[:, :, mine]
        return carry

    lax.fori_loop(0, 3, inverse_z, 0)

    def gather(c, carry):
        to_partner(c).wait_recv()
        vel_ref[c, :, pl.ds(other, 32), :] = recvv[c].astype(F32)
        return carry

    lax.fori_loop(0, 3, gather, 0)

    def finish(c, carry):
        sent(0, c, send1)
        sent(1, c, send2)
        sent(2, c, send3)
        sent(3, c, send4)
        to_partner(c).wait_send()
        return carry

    lax.fori_loop(0, 3, finish, 0)


def spectral(body_force, solid_mask):
    fz, iz = z_tables()
    fx, ix = x_tables()
    ty = y_table()
    any_spec = pl.BlockSpec(memory_space=pl.ANY)
    slab = (3, 16, 2, 32, 128)
    dma = pltpu.SemaphoreType.DMA
    return pl.pallas_call(
        spectral_kernel,
        out_shape=jax.ShapeDtypeStruct((3, 16, 64, 128), F32),
        in_specs=[any_spec] * 7,
        out_specs=pl.BlockSpec(memory_space=pltpu.VMEM),
        scratch_shapes=[
            pltpu.VMEM((3, 16, 32, 256), BF16),
            pltpu.VMEM((16, 32, 256), jnp.int32),
            pltpu.VMEM((256, 256), BF16),
            pltpu.VMEM((256, 256), BF16),
            pltpu.VMEM((512, 1024), BF16),
            pltpu.VMEM((512, 512), BF16),
            pltpu.VMEM((512, 512), BF16),
            pltpu.VMEM((16, 32, 256), F32),
            pltpu.VMEM((1024, 256), BF16),
            pltpu.VMEM((8, 32, 512), BF16),
            pltpu.VMEM((3, 256, 512), F32),
            pltpu.VMEM((3, 256, 512), BF16),
            pltpu.VMEM((16, 32, 256), BF16),
        ]
        + [pltpu.VMEM(slab, BF16)] * 8
        + [pltpu.VMEM((3, 16, 32, 128), BF16)] * 2
        + [dma((7,)), dma((4, 3)), dma((4, 3)), dma((3,)), dma((3,))],
        compiler_params=pltpu.CompilerParams(
            collective_id=0, has_side_effects=True, vmem_limit_bytes=VMEM_LIMIT
        ),
        cost_estimate=pl.CostEstimate(flops=4_000_000_000, bytes_accessed=8_000_000, transcendentals=0),
        name="spectral",
    )(body_force, solid_mask, jnp.asarray(fz), jnp.asarray(iz), jnp.asarray(ty), jnp.asarray(fx), jnp.asarray(ix))


def transport_kernel(
    vel, tracers, inlet, out_ref, state, ysend, yrecv, zsend, zrecv,
    xs_sem, xr_sem, ys_sem, yr_sem, zs_sem, zr_sem,
):
    gx, gy, gz = lax.axis_index("gx"), lax.axis_index("gy"), lax.axis_index("gz")
    x_next, x_last = (gx + 1) % 16, (gx + 15) % 16
    y_next, y_last = (gy + 1) % 8, (gy + 7) % 8
    neighbours = ((x_next, gy, gz), (x_last, gy, gz), (gx, y_next, gz), (gx, y_last, gz), (gx, gy, 1 - gz))

    barrier = pltpu.get_barrier_semaphore()
    for place in neighbours:
        pl.semaphore_signal(barrier, inc=1, device_id=place, device_id_type=MESH)

    for t in range(2):
        state[0, t, 2:18, 8:72, :] = tracers[t]
        injected = jnp.where(inlet[t] == 1, 1.0, tracers[t, 0])
        state[0, t, 2, 8:72, :] = jnp.where(gx == 0, injected, tracers[t, 0])

    pl.semaphore_wait(barrier, 5)
    lane = lax.broadcasted_iota(jnp.int32, (64, 128), 1)

    def copies(step):
        def remote(src, dst, send, recv, place):
            return pltpu.make_async_remote_copy(
                src_ref=src, dst_ref=dst, send_sem=send, recv_sem=recv, device_id=place, device_id_type=MESH
            )

        return (
            remote(state.at[step, :, pl.ds(16, 2), pl.ds(8, 64)], state.at[step, :, pl.ds(0, 2), pl.ds(8, 64)],
                   xs_sem.at[step, 0], xr_sem.at[step, 0], neighbours[0]),
            remote(state.at[step, :, pl.ds(2, 2), pl.ds(8, 64)], state.at[step, :, pl.ds(18, 2), pl.ds(8, 64)],
                   xs_sem.at[step, 1], xr_sem.at[step, 1], neighbours[1]),
            remote(ysend.at[step, 0], yrecv.at[step, 0], ys_sem.at[step, 0], yr_sem.at[step, 0], neighbours[2]),
            remote(ysend.at[step, 1], yrecv.at[step, 1], ys_sem.at[step, 1], yr_sem.at[step, 1], neighbours[3]),
            remote(zsend.at[step], zrecv.at[step], zs_sem.at[step], zr_sem.at[step], neighbours[4]),
        )

    def advance(step, last):
        sends = copies(step)
        sends[0].start()
        sends[1].start()
        for t in range(2):
            for x in range(16):
                row = slice(2 * (x % 4), 2 * (x % 4) + 2)
                ysend[step, 0, t, x // 4, row, :] = state[step, t, 2 + x, 70:72, :]
                ysend[step, 1, t, x // 4, row, :] = state[step, t, 2 + x, 8:10, :]
        sends[2].start()
        sends[3].start()
        packed = jnp.zeros((64, 128), F32)
        for s in range(32):
            edge = pltpu.roll(state[step, s // 16, 2 + s % 16, 8:72, :], (2 + 4 * s) % 128, 1)
            packed = jnp.where(lane // 4 == s, edge, packed)
        zsend[step] = packed
        sends[4].start()
        for send in sends:
            send.wait_recv()
        for t in range(2):
            for x in range(16):
                row = slice(2 * (x % 4), 2 * (x % 4) + 2)
                state[step, t, 2 + x, 6:8, :] = yrecv[step, 0, t, x // 4, row, :]
                state[step, t, 2 + x, 72:74, :] = yrecv[step, 1, t, x // 4, row, :]

        narrow = lax.broadcasted_iota(jnp.int32, (16, 128), 1)

        def plane(x, carry):
            for y in range(0, 64, 16):
                speeds = [vel[d, x, y:y + 16, :] * (-TIME_STEP) for d in range(3)]
                toward = [jnp.minimum(s, 0.0) for s in speeds]
                away = [jnp.maximum(s, 0.0) for s in speeds]
                for t in range(2):
                    rate = TIME_STEP * RATES[t]
                    conc = state[step, t, 2 + x, 8 + y:24 + y, :]

                    def shifted_x(k):
                        return state[step, t, 2 + x + k, 8 + y:24 + y, :]

                    def shifted_y(k):
                        return state[step, t, 2 + x, 8 + y + k:24 + y + k, :]

                    ends = zrecv[step, y:y + 16, :]
                    slot = 4 * (16 * t + x)
                    ends = pltpu.roll(ends, (254 - slot) % 128, 1)
                    wrapped = {-1: narrow == 127, -2: narrow >= 126, 1: narrow == 0, 2: narrow < 2}

                    def shifted_z(k):
                        return pltpu.roll(jnp.where(wrapped[k], ends, conc), -k % 128, 1)

                    total = conc
                    for d, shifted in enumerate((shifted_x, shifted_y, shifted_z)):
                        low, low_two, high, high_two = shifted(-1), shifted(-2), shifted(1), shifted(2)
                        total = total + (1.5 * toward[d] - rate) * (conc - low)
                        total = total - (0.5 * toward[d]) * (low - low_two)
                        total = total + (1.5 * away[d] + rate) * (high - conc)
                        total = total - (0.5 * away[d]) * (high_two - high)
                    if last:
                        out_ref[t, x, y:y + 16, :] = total
                    else:
                        state[step + 1, t, 2 + x, 8 + y:24 + y, :] = total
            return carry

        lax.fori_loop(0, 16, plane, 0)

    def run(step, carry):
        advance(step, False)
        return carry

    lax.fori_loop(0, STEPS - 1, run, 0)
    advance(STEPS - 1, True)

    def finish(step, carry):
        for send in copies(step):
            send.wait_send()
        return carry

    lax.fori_loop(0, STEPS, finish, 0)


def transport(velocity, tracers, inlet_mask):
    vmem = pl.BlockSpec(memory_space=pltpu.VMEM)
    dma = pltpu.SemaphoreType.DMA
    return pl.pallas_call(
        transport_kernel,
        out_shape=jax.ShapeDtypeStruct((2, 16, 64, 128), F32),
        in_specs=[vmem] * 3,
        out_specs=vmem,
        scratch_shapes=[
            pltpu.VMEM((STEPS, 2, 20, 80, 128), F32),
            pltpu.VMEM((STEPS, 2, 2, 4, 8, 128), F32),
            pltpu.VMEM((STEPS, 2, 2, 4, 8, 128), F32),
            pltpu.VMEM((STEPS, 64, 128), F32),
            pltpu.VMEM((STEPS, 64, 128), F32),
            dma((STEPS, 2)), dma((STEPS, 2)), dma((STEPS, 2)), dma((STEPS, 2)), dma((STEPS,)), dma((STEPS,)),
        ],
        compiler_params=pltpu.CompilerParams(
            collective_id=1, has_side_effects=True, vmem_limit_bytes=VMEM_LIMIT
        ),
        cost_estimate=pl.CostEstimate(flops=60_000_000, bytes_accessed=5_000_000, transcendentals=0),
        name="transport",
    )(velocity, tracers, inlet_mask)


def per_device(body_force, solid_mask, tracers, inlet_mask):
    velocity = spectral(body_force, solid_mask)
    return velocity, transport(velocity, tracers, inlet_mask)


def solution(mesh):
    in_specs = (
        P(None, "gx", ("gy", "gz"), None),
        P("gx", ("gy", "gz"), None),
        P(None, "gx", "gy", "gz"),
        P(None, "gy", "gz"),
    )
    out_specs = (P(None, "gx", "gy", "gz"), P(None, "gx", "gy", "gz"))
    return jax.shard_map(per_device, mesh=mesh, in_specs=in_specs, out_specs=out_specs, check_vma=False)
```

time: 595 us -> 116 us (0.19); the launches traced: 584 us -> 115 us
  local copies, waits for them, and re-layouts: 277 us -> 2.76 us
  Pallas kernels: 0 us -> 111 us
  waiting for transfers between devices: 96 us -> 0 us
  other arithmetic: 80.8 us -> 0 us
  starting transfers between devices: 65.6 us -> 0 us
  blocking collectives: 43.4 us -> 0 us
  matrix products: 19.5 us -> 0 us
    pallas_call x0 -> x2, Pallas kernels: none -> 111 us  [the longest x1 72.1 us: spectral(): pl.pallas_call(spectral_kernel, out_shape=jax.ShapeDtypeStruct((3, 16, 64...]
    unnamed x55 -> x6, local copies, waits for them, and re-layouts: 99.6 us -> 2.76 us
    all_to_all x7 -> x0, local copies, waits for them, and re-layouts: 73.5 us -> none  [the longest x1 18.1 us: per_device(): lax.all_to_all(spectrum_y, 'gx', split_axis=4, concat_axis=3, tiled=True)]
    all_to_all x4 -> x0, waiting for transfers between devices: 63.4 us -> none  [the longest x1 36.5 us: per_device(): lax.all_to_all(spectrum_y, 'gx', split_axis=4, concat_axis=3, tiled=True)]
    convert_element_type x5 -> x0, local copies, waits for them, and re-layouts: 57.2 us -> none  [the longest x1 17.4 us: per_device(): rows_y = jnp.einsum('ickxh,ihon->ockxn', lax.all_to_all(back_x, 'gx', spl...]
    convert_element_type x14 -> x0, other arithmetic: 49.6 us -> none  [the longest x4 27.3 us: per_device(): conc.astype(jnp.bfloat16)]
    all_to_all x1 -> x0, blocking collectives: 43.4 us -> none  [per_device(): lax.all_to_all(back_x, 'gx', split_axis=3, concat_axis=4, tiled=True)]
    ppermute x24 -> x0, starting transfers between devices: 35.7 us -> none  [the longest x12 25.8 us: with_halo(): after = lax.ppermute(first, axis, down)]
  transfers between devices with their start and end apart: 28 -> 0, of which waited for: 19 -> 0; matrix products, arithmetic and copies ran while one was open for 6% -> 0% of each run, Pallas kernels for 0% -> 0%
where the time goes in v1:
time: 116 us; the launch traced here: 115 us
  Pallas kernels  111 us (96%)
  local copies, waits for them, and re-layouts  2.76 us (2%)
    pallas_call x1, Pallas kernels, spectral(): pl.pallas_call(spectral_kernel, out_shape=jax.ShapeDtypeStruct((3, 16, 64...  72.1 us
    pallas_call x1, Pallas kernels, transport(): pl.pallas_call(transport_kernel, out_shape=jax.ShapeDtypeStruct((2, 16, 6...  39.1 us
    unnamed x6, local copies, waits for them, and re-layouts  2.76 us

profile of v1, /device:TPU:24, one launch (start us, length us, event | category | flops | bytes accessed | tf_op | source)
XLA Modules:
  0.0 114.6 jit_solution(445409332982947331)
XLA Ops:
  0.6 72.1 %spectral.1.vel = f32[3,16,64,128]{3,2,1,0:T(8,128)} custom-call(bf16[3,16,32,256]{3,2,1,0:T(8,128)(2,1)} %force_hbm.1, s32[16,32,256]{2,1,0:T(8,128)} %mask_hbm.1, bf16[256,256]{1,0:T(8,128)(2,1)} %constant.10.clone.fz_hbm, bf16[256,256]{1,0:T(8,128)(2,1)} %constant.11.clone.iz_hbm, bf16[512,1024]{1,0:T(8,128)(2,1)} %constant.12.clone.ty_hbm, ...), custom_call_target="tpu_custom_call" | custom-call | flops 4000000000 | bytes 8000000 | tf_op jit(solution)/shard_map/spectral/pallas_call | solution.py:299
  72.7 0.0 copy-start
  72.7 39.1 %transport.1 = f32[2,16,64,128]{3,2,1,0:T(8,128)} custom-call(f32[3,16,64,128]{3,2,1,0:T(8,128)} %spectral.1.vel, f32[2,16,64,128]{3,2,1,0:T(8,128)} %tracers.1, s32[2,64,128]{2,1,0:T(8,128)} %inlet.1), custom_call_target="tpu_custom_call" | custom-call | flops 60000000 | bytes 5000000 | tf_op jit(solution)/shard_map/transport/pallas_call | solution.py:450
  111.8 0.0 copy-done
  111.8 0.0 copy-start.1
  111.8 1.1 copy.13
  113.0 0.6 copy-done.1
  113.6 1.0 copy.14
Async XLA Ops:
  72.7 39.1 %copy-start = (f32[3,16,64,128]{3,2,1,0:T(8,128)S(1)}, f32[3,16,64,128]{3,2,1,0:T(8,128)}, u32[]{:S(2)}) copy-start(f32[3,16,64,128]{3,2,1,0:T(8,128)} %spectral.1.vel) | copy-start | bytes 4718596
  111.8 1.8 %copy-start.1 = (f32[2,16,64,128]{3,2,1,0:T(8,128)S(1)}, f32[2,16,64,128]{3,2,1,0:T(8,128)}, u32[]{:S(2)}) copy-start(f32[2,16,64,128]{3,2,1,0:T(8,128)} %transport.1) | copy-start | bytes 3145732

commit v2 on v1

--- a/solution.py
+++ b/solution.py
@@ -1,4 +1,3 @@
-import functools
 import math
 
 import jax
@@ -77,11 +76,16 @@
     return signed.astype(F32) * (2.0 * math.pi / length)
 
 
-def spectral_kernel(
-    force_hbm, mask_hbm, fz_hbm, iz_hbm, ty_hbm, fx_hbm, ix_hbm, vel_ref,
+TILES = ((0, 1, 14, 15), (2, 3, 4, 5), (6, 7, 8, 9), (10, 11, 12, 13))
+GROUPS = ((0, 1), (1, 1), (2, 2))
+
+
+def fused_kernel(
+    force_hbm, mask_hbm, tracers_hbm, inlet_hbm, fz_hbm, iz_hbm, ty_hbm, fx_hbm, ix_hbm, vel_ref, out_ref,
     force, mask, fz, iz, ty, fx, ix, zbuf, rhs, xin, spec, green, zin,
     send1, recv1, send2, recv2, send3, recv3, send4, recv4, sendv, recvv,
-    load_sem, send_sem, recv_sem, vsend_sem, vrecv_sem,
+    inlet, state, ends, stage, xsend, xrecv, ysend, yrecv, zsend, zrecv,
+    load_sem, send_sem, recv_sem, vsend_sem, vrecv_sem, xs_sem, xr_sem, fs_sem, fr_sem,
 ):
     gx, gy, gz = lax.axis_index("gx"), lax.axis_index("gy"), lax.axis_index("gz")
     group = gy * 2 + gz
@@ -95,7 +99,8 @@
     loads = [
         pltpu.make_async_copy(src, dst, load_sem.at[n])
         for n, (src, dst) in enumerate(
-            [(fz_hbm, fz), (mask_hbm, mask), (force_hbm, force), (ty_hbm, ty), (fx_hbm, fx), (ix_hbm, ix), (iz_hbm, iz)]
+            [(fz_hbm, fz), (mask_hbm, mask), (force_hbm, force), (ty_hbm, ty), (fx_hbm, fx), (ix_hbm, ix), (iz_hbm, iz),
+             (inlet_hbm, inlet), (tracers_hbm, state.at[0, :, pl.ds(2, 16), pl.ds(8, 64)])]
         )
     ]
     for load in loads:
@@ -176,6 +181,15 @@
         return carry
 
     lax.fori_loop(0, 3, forward_y, 0)
+
+    halo = Halo(state, ends, stage, xsend, xrecv, ysend, yrecv, zsend, zrecv, xs_sem, xr_sem, fs_sem, fr_sem)
+    loads[7].wait()
+    loads[8].wait()
+    for t in range(2):
+        plane = state[0, t, 2, 8:72, :]
+        state[0, t, 2, 8:72, :] = jnp.where(gx == 0, jnp.where(inlet[t] == 1, 1.0, plane), plane)
+    for group_id in range(3):
+        halo.send(0, group_id)
 
     loads[4].wait()
 
@@ -278,6 +292,8 @@
 
     lax.fori_loop(0, 3, gather, 0)
 
+    transport(vel_ref, out_ref, halo)
+
     def finish(c, carry):
         sent(0, c, send1)
         sent(1, c, send2)
@@ -289,18 +305,176 @@
     lax.fori_loop(0, 3, finish, 0)
 
 
-def spectral(body_force, solid_mask):
+class Halo:
+    def __init__(self, state, ends, stage, xsend, xrecv, ysend, yrecv, zsend, zrecv, xs_sem, xr_sem, fs_sem, fr_sem):
+        self.state, self.ends, self.stage = state, ends, stage
+        self.xsend, self.xrecv, self.ysend, self.yrecv = xsend, xrecv, ysend, yrecv
+        self.zsend, self.zrecv = zsend, zrecv
+        self.xs_sem, self.xr_sem, self.fs_sem, self.fr_sem = xs_sem, xr_sem, fs_sem, fr_sem
+
+    def copies(self, step, group_id):
+        gx, gy, gz = lax.axis_index("gx"), lax.axis_index("gy"), lax.axis_index("gz")
+
+        def remote(src, dst, send, recv, place):
+            return pltpu.make_async_remote_copy(
+                src_ref=src, dst_ref=dst, send_sem=send, recv_sem=recv, device_id=place, device_id_type=MESH
+            )
+
+        tiles = pl.ds(*GROUPS[group_id])
+        found = [
+            remote(self.ysend.at[step, side, tiles], self.yrecv.at[step, side, tiles],
+                   self.fs_sem.at[step, group_id, side], self.fr_sem.at[step, group_id, side], place)
+            for side, place in enumerate(((gx, (gy + 1) % 8, gz), (gx, (gy + 7) % 8, gz)))
+        ]
+        found.append(
+            remote(self.zsend.at[step, tiles], self.zrecv.at[step, tiles],
+                   self.fs_sem.at[step, group_id, 2], self.fr_sem.at[step, group_id, 2], (gx, gy, 1 - gz))
+        )
+        if group_id == 0:
+            found += [
+                remote(self.xsend.at[step, side], self.xrecv.at[step, side],
+                       self.xs_sem.at[step, side], self.xr_sem.at[step, side], place)
+                for side, place in enumerate((((gx + 1) % 16, gy, gz), ((gx + 15) % 16, gy, gz)))
+            ]
+        return found
+
+    def send(self, step, group_id):
+        state = self.state
+        first, count = GROUPS[group_id]
+        copies = self.copies(step, group_id)
+        if group_id == 0:
+            self.xsend[step, 0] = state[step, :, 16:18, 8:72, :].astype(BF16)
+            self.xsend[step, 1] = state[step, :, 2:4, 8:72, :].astype(BF16)
+            copies[3].start()
+            copies[4].start()
+        slot = lax.broadcasted_iota(jnp.int32, (16, 128), 1) // 4
+        for tile in range(first, first + count):
+            packed = jnp.zeros((16, 128), F32)
+            for t in range(2):
+                for i, x in enumerate(TILES[tile]):
+                    slab = 4 * t + i
+                    self.stage[0, 2 * slab:2 * slab + 2, :] = state[step, t, 2 + x, 70:72, :]
+                    self.stage[1, 2 * slab:2 * slab + 2, :] = state[step, t, 2 + x, 8:10, :]
+                    for b in range(4):
+                        edge = pltpu.roll(
+                            state[step, t, 2 + x, 8 + 16 * b:24 + 16 * b, :], (2 + 32 * b + 4 * slab) % 128, 1
+                        )
+                        packed = jnp.where(slot == 8 * b + slab, edge, packed)
+            self.ysend[step, 0, tile] = self.stage[0].astype(BF16)
+            self.ysend[step, 1, tile] = self.stage[1].astype(BF16)
+            self.zsend[step, tile] = packed.astype(BF16)
+        for copy in copies[:3]:
+            copy.start()
+
+    def receive(self, step, group_id):
+        state = self.state
+        first, count = GROUPS[group_id]
+        for copy in self.copies(step, group_id):
+            copy.wait_recv()
+        if group_id == 0:
+            state[step, :, 0:2, 8:72, :] = self.xrecv[step, 0].astype(F32)
+            state[step, :, 18:20, 8:72, :] = self.xrecv[step, 1].astype(F32)
+        for tile in range(first, first + count):
+            self.stage[0] = self.yrecv[step, 0, tile].astype(F32)
+            self.stage[1] = self.yrecv[step, 1, tile].astype(F32)
+            packed = self.zrecv[step, tile].astype(F32)
+            for t in range(2):
+                for i, x in enumerate(TILES[tile]):
+                    slab = 4 * t + i
+                    state[step, t, 2 + x, 6:8, :] = self.stage[0, 2 * slab:2 * slab + 2, :]
+                    state[step, t, 2 + x, 72:74, :] = self.stage[1, 2 * slab:2 * slab + 2, :]
+                    for b in range(4):
+                        self.ends[t, x, 16 * b:16 * b + 16, :] = pltpu.roll(
+                            packed, (254 - 32 * b - 4 * slab) % 128, 1
+                        )
+
+
+def transport(vel, out_ref, halo):
+    state = halo.state
+    lane = lax.broadcasted_iota(jnp.int32, (16, 128), 1)
+    wrapped = {-1: lane == 127, -2: lane >= 126, 1: lane == 0, 2: lane < 2}
+
+    def compute(step, group_id, last):
+        first, count = GROUPS[group_id]
+
+        def plane(n, carry):
+            x = n + jnp.where(n >= 2, 12, 0) if group_id == 0 else TILES[first][0] + n
+            for y in range(0, 64, 16):
+                speeds = [vel[d, x, y:y + 16, :] * (-TIME_STEP) for d in range(3)]
+                upward = [s < 0.0 for s in speeds]
+                one = [1.5 * s for s in speeds]
+                two = [0.5 * s for s in speeds]
+                for t in range(2):
+                    conc = state[step, t, 2 + x, 8 + y:24 + y, :]
+                    edge = halo.ends[t, x, y:y + 16, :]
+
+                    def shifted_x(k):
+                        return state[step, t, 2 + x + k, 8 + y:24 + y, :]
+
+                    def shifted_y(k):
+                        return state[step, t, 2 + x, 8 + y + k:24 + y + k, :]
+
+                    def shifted_z(k):
+                        return pltpu.roll(jnp.where(wrapped[k], edge, conc), -k % 128, 1)
+
+                    total = conc
+                    laplace = None
+                    for d, shifted in enumerate((shifted_x, shifted_y, shifted_z)):
+                        low, low_two, high, high_two = shifted(-1), shifted(-2), shifted(1), shifted(2)
+                        below, above = conc - low, high - conc
+                        near = jnp.where(upward[d], below, above)
+                        far = jnp.where(upward[d], low - low_two, high_two - high)
+                        total = total + one[d] * near - two[d] * far
+                        bend = above - below
+                        laplace = bend if laplace is None else laplace + bend
+                    total = total + (TIME_STEP * RATES[t]) * laplace
+                    if last:
+                        out_ref[t, x, y:y + 16, :] = total
+                    else:
+                        state[step + 1, t, 2 + x, 8 + y:24 + y, :] = total
+            return carry
+
+        lax.fori_loop(0, 4 * count, plane, 0)
+
+    def advance(step, last):
+        for group_id in range(3):
+            halo.receive(step, group_id)
+            compute(step, group_id, last)
+            if not last:
+                halo.send(step + 1, group_id)
+
+    def run(step, carry):
+        advance(step, False)
+        return carry
+
+    lax.fori_loop(0, STEPS - 1, run, 0)
+    advance(STEPS - 1, True)
+
+    def finish(step, carry):
+        for group_id in range(3):
+            for copy in halo.copies(step, group_id):
+                copy.wait_send()
+        return carry
+
+    lax.fori_loop(0, STEPS, finish, 0)
+
+
+def fused(body_force, solid_mask, tracers, inlet_mask):
     fz, iz = z_tables()
     fx, ix = x_tables()
     ty = y_table()
     any_spec = pl.BlockSpec(memory_space=pl.ANY)
+    vmem = pl.BlockSpec(memory_space=pltpu.VMEM)
     slab = (3, 16, 2, 32, 128)
     dma = pltpu.SemaphoreType.DMA
     return pl.pallas_call(
-        spectral_kernel,
-        out_shape=jax.ShapeDtypeStruct((3, 16, 64, 128), F32),
-        in_specs=[any_spec] * 7,
-        out_specs=pl.BlockSpec(memory_space=pltpu.VMEM),
+        fused_kernel,
+        out_shape=(
+            jax.ShapeDtypeStruct((3, 16, 64, 128), F32),
+            jax.ShapeDtypeStruct((2, 16, 64, 128), F32),
+        ),
+        in_specs=[any_spec] * 9,
+        out_specs=(vmem, vmem),
         scratch_shapes=[
             pltpu.VMEM((3, 16, 32, 256), BF16),
             pltpu.VMEM((16, 32, 256), jnp.int32),
@@ -318,159 +492,25 @@
         ]
         + [pltpu.VMEM(slab, BF16)] * 8
         + [pltpu.VMEM((3, 16, 32, 128), BF16)] * 2
-        + [dma((7,)), dma((4, 3)), dma((4, 3)), dma((3,)), dma((3,))],
+        + [
+            pltpu.VMEM((2, 64, 128), jnp.int32),
+            pltpu.VMEM((STEPS, 2, 20, 80, 128), F32),
+            pltpu.VMEM((2, 16, 64, 128), F32),
+            pltpu.VMEM((2, 16, 128), F32),
+        ]
+        + [pltpu.VMEM((STEPS, 2, 2, 2, 64, 128), BF16)] * 2
+        + [pltpu.VMEM((STEPS, 2, 4, 16, 128), BF16)] * 2
+        + [pltpu.VMEM((STEPS, 4, 16, 128), BF16)] * 2
+        + [dma((9,)), dma((4, 3)), dma((4, 3)), dma((3,)), dma((3,))]
+        + [dma((STEPS, 2)), dma((STEPS, 2)), dma((STEPS, 3, 3)), dma((STEPS, 3, 3))],
         compiler_params=pltpu.CompilerParams(
             collective_id=0, has_side_effects=True, vmem_limit_bytes=VMEM_LIMIT
         ),
-        cost_estimate=pl.CostEstimate(flops=4_000_000_000, bytes_accessed=8_000_000, transcendentals=0),
-        name="spectral",
-    )(body_force, solid_mask, jnp.asarray(fz), jnp.asarray(iz), jnp.asarray(ty), jnp.asarray(fx), jnp.asarray(ix))
-
-
-def transport_kernel(
-    vel, tracers, inlet, out_ref, state, ysend, yrecv, zsend, zrecv,
-    xs_sem, xr_sem, ys_sem, yr_sem, zs_sem, zr_sem,
-):
-    gx, gy, gz = lax.axis_index("gx"), lax.axis_index("gy"), lax.axis_index("gz")
-    x_next, x_last = (gx + 1) % 16, (gx + 15) % 16
-    y_next, y_last = (gy + 1) % 8, (gy + 7) % 8
-    neighbours = ((x_next, gy, gz), (x_last, gy, gz), (gx, y_next, gz), (gx, y_last, gz), (gx, gy, 1 - gz))
-
-    barrier = pltpu.get_barrier_semaphore()
-    for place in neighbours:
-        pl.semaphore_signal(barrier, inc=1, device_id=place, device_id_type=MESH)
-
-    for t in range(2):
-        state[0, t, 2:18, 8:72, :] = tracers[t]
-        injected = jnp.where(inlet[t] == 1, 1.0, tracers[t, 0])
-        state[0, t, 2, 8:72, :] = jnp.where(gx == 0, injected, tracers[t, 0])
-
-    pl.semaphore_wait(barrier, 5)
-    lane = lax.broadcasted_iota(jnp.int32, (64, 128), 1)
-
-    def copies(step):
-        def remote(src, dst, send, recv, place):
-            return pltpu.make_async_remote_copy(
-                src_ref=src, dst_ref=dst, send_sem=send, recv_sem=recv, device_id=place, device_id_type=MESH
-            )
-
-        return (
-            remote(state.at[step, :, pl.ds(16, 2), pl.ds(8, 64)], state.at[step, :, pl.ds(0, 2), pl.ds(8, 64)],
-                   xs_sem.at[step, 0], xr_sem.at[step, 0], neighbours[0]),
-            remote(state.at[step, :, pl.ds(2, 2), pl.ds(8, 64)], state.at[step, :, pl.ds(18, 2), pl.ds(8, 64)],
-                   xs_sem.at[step, 1], xr_sem.at[step, 1], neighbours[1]),
-            remote(ysend.at[step, 0], yrecv.at[step, 0], ys_sem.at[step, 0], yr_sem.at[step, 0], neighbours[2]),
-            remote(ysend.at[step, 1], yrecv.at[step, 1], ys_sem.at[step, 1], yr_sem.at[step, 1], neighbours[3]),
-            remote(zsend.at[step], zrecv.at[step], zs_sem.at[step], zr_sem.at[step], neighbours[4]),
-        )
-
-    def advance(step, last):
-        sends = copies(step)
-        sends[0].start()
-        sends[1].start()
-        for t in range(2):
-            for x in range(16):
-                row = slice(2 * (x % 4), 2 * (x % 4) + 2)
-                ysend[step, 0, t, x // 4, row, :] = state[step, t, 2 + x, 70:72, :]
-                ysend[step, 1, t, x // 4, row, :] = state[step, t, 2 + x, 8:10, :]
-        sends[2].start()
-        sends[3].start()
-        packed = jnp.zeros((64, 128), F32)
-        for s in range(32):
-            edge = pltpu.roll(state[step, s // 16, 2 + s % 16, 8:72, :], (2 + 4 * s) % 128, 1)
-            packed = jnp.where(lane // 4 == s, edge, packed)
-        zsend[step] = packed
-        sends[4].start()
-        for send in sends:
-            send.wait_recv()
-        for t in range(2):
-            for x in range(16):
-                row = slice(2 * (x % 4), 2 * (x % 4) + 2)
-                state[step, t, 2 + x, 6:8, :] = yrecv[step, 0, t, x // 4, row, :]
-                state[step, t, 2 + x, 72:74, :] = yrecv[step, 1, t, x // 4, row, :]
-
-        narrow = lax.broadcasted_iota(jnp.int32, (16, 128), 1)
-
-        def plane(x, carry):
-            for y in range(0, 64, 16):
-                speeds = [vel[d, x, y:y + 16, :] * (-TIME_STEP) for d in range(3)]
-                toward = [jnp.minimum(s, 0.0) for s in speeds]
-                away = [jnp.maximum(s, 0.0) for s in speeds]
-                for t in range(2):
-                    rate = TIME_STEP * RATES[t]
-                    conc = state[step, t, 2 + x, 8 + y:24 + y, :]
-
-                    def shifted_x(k):
-                        return state[step, t, 2 + x + k, 8 + y:24 + y, :]
-
-                    def shifted_y(k):
-                        return state[step, t, 2 + x, 8 + y + k:24 + y + k, :]
-
-                    ends = zrecv[step, y:y + 16, :]
-                    slot = 4 * (16 * t + x)
-                    ends = pltpu.roll(ends, (254 - slot) % 128, 1)
-                    wrapped = {-1: narrow == 127, -2: narrow >= 126, 1: narrow == 0, 2: narrow < 2}
-
-                    def shifted_z(k):
-                        return pltpu.roll(jnp.where(wrapped[k], ends, conc), -k % 128, 1)
-
-                    total = conc
-                    for d, shifted in enumerate((shifted_x, shifted_y, shifted_z)):
-                        low, low_two, high, high_two = shifted(-1), shifted(-2), shifted(1), shifted(2)
-                        total = total + (1.5 * toward[d] - rate) * (conc - low)
-                        total = total - (0.5 * toward[d]) * (low - low_two)
-                        total = total + (1.5 * away[d] + rate) * (high - conc)
-                        total = total - (0.5 * away[d]) * (high_two - high)
-                    if last:
-                        out_ref[t, x, y:y + 16, :] = total
-                    else:
-                        state[step + 1, t, 2 + x, 8 + y:24 + y, :] = total
-            return carry
-
-        lax.fori_loop(0, 16, plane, 0)
-
-    def run(step, carry):
-        advance(step, False)
-        return carry
-
-    lax.fori_loop(0, STEPS - 1, run, 0)
-    advance(STEPS - 1, True)
-
-    def finish(step, carry):
-        for send in copies(step):
-            send.wait_send()
-        return carry
-
-    lax.fori_loop(0, STEPS, finish, 0)
-
-
-def transport(velocity, tracers, inlet_mask):
-    vmem = pl.BlockSpec(memory_space=pltpu.VMEM)
-    dma = pltpu.SemaphoreType.DMA
-    return pl.pallas_call(
-        transport_kernel,
-        out_shape=jax.ShapeDtypeStruct((2, 16, 64, 128), F32),
-        in_specs=[vmem] * 3,
-        out_specs=vmem,
-        scratch_shapes=[
-            pltpu.VMEM((STEPS, 2, 20, 80, 128), F32),
-            pltpu.VMEM((STEPS, 2, 2, 4, 8, 128), F32),
-            pltpu.VMEM((STEPS, 2, 2, 4, 8, 128), F32),
-            pltpu.VMEM((STEPS, 64, 128), F32),
-            pltpu.VMEM((STEPS, 64, 128), F32),
-            dma((STEPS, 2)), dma((STEPS, 2)), dma((STEPS, 2)), dma((STEPS, 2)), dma((STEPS,)), dma((STEPS,)),
-        ],
-        compiler_params=pltpu.CompilerParams(
-            collective_id=1, has_side_effects=True, vmem_limit_bytes=VMEM_LIMIT
-        ),
-        cost_estimate=pl.CostEstimate(flops=60_000_000, bytes_accessed=5_000_000, transcendentals=0),
-        name="transport",
-    )(velocity, tracers, inlet_mask)
-
-
-def per_device(body_force, solid_mask, tracers, inlet_mask):
-    velocity = spectral(body_force, solid_mask)
-    return velocity, transport(velocity, tracers, inlet_mask)
+        name="stokes_transport",
+    )(
+        body_force, solid_mask, tracers, inlet_mask,
+        jnp.asarray(fz), jnp.asarray(iz), jnp.asarray(ty), jnp.asarray(fx), jnp.asarray(ix),
+    )
 
 
 def solution(mesh):
@@ -481,4 +521,4 @@
         P(None, "gy", "gz"),
     )
     out_specs = (P(None, "gx", "gy", "gz"), P(None, "gx", "gy", "gz"))
-    return jax.shard_map(per_device, mesh=mesh, in_specs=in_specs, out_specs=out_specs, check_vma=False)
+    return jax.shard_map(fused, mesh=mesh, in_specs=in_specs, out_specs=out_specs, check_vma=False)

time: 116 us -> 99.1 us (0.85); the launches traced: 115 us -> 98.9 us
  Pallas kernels: 111 us -> 94.5 us
    pallas_call x2 -> x1, Pallas kernels: 111 us -> 94.5 us  [fused(): pl.pallas_call(fused_kernel, out_shape=(jax.ShapeDtypeStruct((3, 16, 64,...]
    unnamed x6 -> x4, local copies, waits for them, and re-layouts: 2.76 us -> 3.79 us
where the time goes in v2:
time: 99.1 us; the launch traced here: 98.9 us
  Pallas kernels  94.5 us (95%)
  local copies, waits for them, and re-layouts  3.79 us (4%)
    pallas_call x1, Pallas kernels, fused(): pl.pallas_call(fused_kernel, out_shape=(jax.ShapeDtypeStruct((3, 16, 64,...  94.5 us
    unnamed x4, local copies, waits for them, and re-layouts  3.79 us

profile of v2, /device:TPU:24, one launch (start us, length us, event | category | flops | bytes accessed | tf_op | source)
XLA Modules:
  0.0 98.9 jit_solution(926118365855970963)
XLA Ops:
  0.6 94.5 %stokes_transport.1 = (f32[3,16,64,128]{3,2,1,0:T(8,128)}, f32[2,16,64,128]{3,2,1,0:T(8,128)}) custom-call(bf16[3,16,32,256]{3,2,1,0:T(8,128)(2,1)} %force_hbm.1, s32[16,32,256]{2,1,0:T(8,128)} %mask_hbm.1, f32[2,16,64,128]{3,2,1,0:T(8,128)} %tracers_hbm.1, s32[2,64,128]{2,1,0:T(8,128)} %inlet_hbm.1, bf16[256,256]{1,0:T(8,128)(2,1)} %constant.10.clone.fz_hbm, ...), custom_call_target="tpu_custom_call" | custom-call | tf_op jit(solution)/shard_map/stokes_transport/pallas_call | solution.py:470
  95.1 0.0 copy-start
  95.2 2.8 %copy.13 = f32[3,16,64,128]{3,2,1,0:T(8,128)} copy(f32[3,16,64,128]{3,2,1,0:T(8,128)} %get-tuple-element.4) | data formatting | bytes 3145728
  98.0 0.0 copy-done
  98.0 1.0 copy.14
Async XLA Ops:
  95.1 2.8 %copy-start = (f32[2,16,64,128]{3,2,1,0:T(8,128)S(1)}, f32[2,16,64,128]{3,2,1,0:T(8,128)}, u32[]{:S(2)}) copy-start(f32[2,16,64,128]{3,2,1,0:T(8,128)} %get-tuple-element.5) | copy-start | bytes 3145732

commit v3 on v2

--- a/solution.py
+++ b/solution.py
@@ -115,24 +115,24 @@
 
     lax.fori_loop(1, 16, greet, 0)
 
-    def exchange(stage, c, send, recv, me, place):
+    def exchange(row, c, n, send, recv, me, place):
         def one(k, carry):
             to = (me + k) % 16
             pltpu.make_async_remote_copy(
-                src_ref=send.at[c, to], dst_ref=recv.at[c, me],
-                send_sem=send_sem.at[stage, c], recv_sem=recv_sem.at[stage, c],
+                src_ref=send.at[n, to], dst_ref=recv.at[n, me],
+                send_sem=send_sem.at[row, c], recv_sem=recv_sem.at[row, c],
                 device_id=place(to), device_id_type=MESH,
             ).start()
             return carry
 
         lax.fori_loop(1, 16, one, 0)
-        pltpu.make_async_copy(send.at[c, me], recv.at[c, me], recv_sem.at[stage, c]).start()
-
-    def arrived(stage, c, recv):
-        pltpu.make_async_copy(recv.at[c], recv.at[c], recv_sem.at[stage, c]).wait()
-
-    def sent(stage, c, send):
-        pltpu.make_async_copy(send.at[c, pl.ds(0, 15)], send.at[c, pl.ds(0, 15)], send_sem.at[stage, c]).wait()
+        pltpu.make_async_copy(send.at[n, me], recv.at[n, me], recv_sem.at[row, c]).start()
+
+    def arrived(row, c, n, recv):
+        pltpu.make_async_copy(recv.at[n], recv.at[n], recv_sem.at[row, c]).wait()
+
+    def sent(row, c, n, send):
+        pltpu.make_async_copy(send.at[n, pl.ds(0, 15)], send.at[n, pl.ds(0, 15)], send_sem.at[row, c]).wait()
 
     for load in loads[:3]:
         load.wait()
@@ -142,45 +142,51 @@
             rows = slice(8 * h, 8 * h + 8)
             kept = jnp.where(mask[rows] == 0, force[c, rows].astype(F32), 0.0).astype(BF16)
             out = jnp.dot(kept.reshape(256, 256), fz[...], preferred_element_type=F32)
-            zbuf[rows] = out.reshape(8, 32, 256)
+            zin[rows] = out.astype(BF16).reshape(8, 32, 256)
         for ri in range(2):
             for y in (0, 16):
-                parts = [zbuf[x, y:y + 16, 128 * ri:128 * ri + 128] for x in range(16)]
+                parts = [zin[x, y:y + 16, 128 * ri:128 * ri + 128] for x in range(16)]
                 parts = swap_index_and_lanes(parts, 8)
                 for to in range(16):
-                    send1[c, to, ri, y:y + 16, :] = parts[to].astype(BF16)
+                    send1[c, to, ri, y:y + 16, :] = parts[to]
 
         @pl.when(c == 0)
         def _():
             pl.semaphore_wait(barrier, 30)
 
-        exchange(0, c, send1, recv1, group, in_plane)
+        exchange(0, c, c, send1, recv1, group, in_plane)
         return carry
 
     lax.fori_loop(0, 3, forward_z, 0)
 
-    def y_transform(recv, send, c, forward):
-        re = recv[c, :, 0].reshape(512, 128)
-        im = recv[c, :, 1].reshape(512, 128)
-        rhs[0:512, 0:128] = re
-        rhs[0:512, 128:256] = im
-        rhs[512:1024, 0:128] = im if forward else -im
-        rhs[512:1024, 128:256] = -re if forward else re
-        for h in range(2):
-            out = jnp.dot(ty[256 * h:256 * h + 256, :], rhs[...], preferred_element_type=F32)
-            out = out.astype(BF16).reshape(8, 32, 256)
-            send[c, 8 * h:8 * h + 8, 0] = out[:, :, 0:128]
-            send[c, 8 * h:8 * h + 8, 1] = out[:, :, 128:256]
-
     loads[3].wait()
 
     def forward_y(c, carry):
-        arrived(0, c, recv1)
-        y_transform(recv1, send2, c, True)
-        exchange(1, c, send2, recv2, gx, in_column)
+        arrived(0, c, c, recv1)
+        re = recv1[c, :, 0].reshape(16, 2, 16, 128)
+        im = recv1[c, :, 1].reshape(16, 2, 16, 128)
+        rhs[0, :, :, :, 0:128] = re
+        rhs[0, :, :, :, 128:256] = im
+        rhs[1, :, :, :, 0:128] = im
+        rhs[1, :, :, :, 128:256] = -re
+        for m in range(2):
+            out = jnp.dot(
+                ty[256 * m:256 * m + 256, :], rhs[...].reshape(1024, 256), preferred_element_type=F32
+            )
+            out = out.astype(BF16).reshape(8, 2, 16, 256)
+            for h in range(2):
+                for ro in range(2):
+                    send2[3 * h + c, 8 * m:8 * m + 8, ro] = out[:, h, :, 128 * ro:128 * ro + 128]
+        exchange(1, c, c, send2, recv2, gx, in_column)
         return carry
 
     lax.fori_loop(0, 3, forward_y, 0)
+
+    def second_half(c, carry):
+        exchange(2, c, 3 + c, send2, recv2, gx, in_column)
+        return carry
+
+    lax.fori_loop(0, 3, second_half, 0)
 
     halo = Halo(state, ends, stage, xsend, xrecv, ysend, yrecv, zsend, zrecv, xs_sem, xr_sem, fs_sem, fr_sem)
     loads[7].wait()
@@ -192,64 +198,79 @@
         halo.send(0, group_id)
 
     loads[4].wait()
-
-    def forward_x(c, carry):
-        arrived(1, c, recv2)
-        for ri in range(2):
-            for hi in range(2):
-                for ky in (0, 16):
-                    parts = [recv2[c, 8 * hi + i, ri, ky:ky + 16, :].astype(F32) for i in range(8)]
-                    parts = swap_index_and_lanes(parts, 1)
-                    lanes = slice(256 * ri + 128 * hi, 256 * ri + 128 * hi + 128)
-                    for k in range(8):
-                        xin[k, ky:ky + 16, lanes] = parts[k].astype(BF16)
-        spec[c] = jnp.dot(xin[...].reshape(256, 512), fx[...], preferred_element_type=F32)
-        return carry
-
-    lax.fori_loop(0, 3, forward_x, 0)
-
+    loads[5].wait()
     wave_x = signed_wave(lax.broadcasted_iota(jnp.int32, (16, GRID_X), 1), GRID_X)
     row = lax.broadcasted_iota(jnp.int32, (16, GRID_X), 0)
 
-    def project(b, carry):
-        at = pl.ds(pl.multiple_of(b * 16, 16), 16)
-        wave_y = signed_wave(gx * 32 + (b % 2) * 16 + row, GRID_Y)
-        wave_z = signed_wave(group * 8 + b // 2 + jnp.zeros_like(row), GRID_Z)
-        wave_sq = wave_x * wave_x + wave_y * wave_y + wave_z * wave_z
-        gain = 1.0 / ((VISCOSITY * wave_sq + SCREENING) * float(GRID_X * GRID_Y * GRID_Z))
-        inverse_sq = jnp.where(wave_sq > 0, 1.0 / jnp.where(wave_sq > 0, wave_sq, 1.0), 0.0)
-        waves = (wave_x, wave_y, wave_z)
-        for lanes in (slice(0, 256), slice(256, 512)):
-            parts = [spec[c, at, lanes] for c in range(3)]
-            inner = waves[0] * parts[0] + waves[1] * parts[1] + waves[2] * parts[2]
-            along = inner * inverse_sq
-            for c in range(3):
-                green[c, at, lanes] = (gain * (parts[c] - waves[c] * along)).astype(BF16)
-        return carry
-
-    lax.fori_loop(0, 16, project, 0)
-
-    loads[5].wait()
-
-    def inverse_x(c, carry):
-        spec[c] = jnp.dot(green[c], ix[...], preferred_element_type=F32)
-        for ro in range(2):
-            for hi in range(2):
-                for ky in (0, 16):
+    def middle(h, carry):
+        def forward_x(c, carry):
+            n = 3 * h + c
+            arrived(1 + h, c, n, recv2)
+            for ri in range(2):
+                for hi in range(2):
+                    parts = [recv2[n, 8 * hi + i, ri] for i in range(8)]
+                    parts = swap_index_and_lanes(parts, 1)
+                    first = 256 * ri + 128 * hi
+                    for k in range(8):
+                        xin[c, k, :, first:first + 128] = parts[k]
+            return carry
+
+        lax.fori_loop(0, 3, forward_x, 0)
+        spec[...] = jnp.dot(xin[...].reshape(384, 512), fx[...], preferred_element_type=F32).reshape(3, 8, 16, 512)
+
+        def project(k, carry):
+            wave_y = signed_wave(gx * 32 + h * 16 + row, GRID_Y)
+            wave_z = signed_wave(group * 8 + k + jnp.zeros_like(row), GRID_Z)
+            wave_sq = wave_x * wave_x + wave_y * wave_y + wave_z * wave_z
+            gain = 1.0 / ((VISCOSITY * wave_sq + SCREENING) * float(GRID_X * GRID_Y * GRID_Z))
+            inverse_sq = jnp.where(wave_sq > 0, 1.0 / jnp.where(wave_sq > 0, wave_sq, 1.0), 0.0)
+            waves = (wave_x, wave_y, wave_z)
+            for lanes in (slice(0, 256), slice(256, 512)):
+                parts = [spec[c, k, :, lanes] for c in range(3)]
+                inner = waves[0] * parts[0] + waves[1] * parts[1] + waves[2] * parts[2]
+                along = inner * inverse_sq
+                for c in range(3):
+                    green[c, k, :, lanes] = (gain * (parts[c] - waves[c] * along)).astype(BF16)
+            return carry
+
+        lax.fori_loop(0, 8, project, 0)
+        back = jnp.dot(green[...].reshape(384, 512), ix[...], preferred_element_type=F32)
+        xin[...] = back.astype(BF16).reshape(3, 8, 16, 512)
+
+        def inverse_x(c, carry):
+            n = 3 * h + c
+            for ro in range(2):
+                for hi in range(2):
                     first = 256 * ro + 128 * hi
-                    parts = [spec[c, 32 * k + ky:32 * k + ky + 16, first:first + 128] for k in range(8)]
+                    parts = [xin[c, k, :, first:first + 128] for k in range(8)]
                     parts = swap_index_and_lanes(parts, 1)
                     for i in range(8):
-                        send3[c, 8 * hi + i, ro, ky:ky + 16, :] = parts[i].astype(BF16)
-        exchange(2, c, send3, recv3, gx, in_column)
-        return carry
-
-    lax.fori_loop(0, 3, inverse_x, 0)
+                        send3[n, 8 * hi + i, ro] = parts[i]
+            exchange(3 + h, c, n, send3, recv3, gx, in_column)
+            return carry
+
+        lax.fori_loop(0, 3, inverse_x, 0)
+        return carry
+
+    lax.fori_loop(0, 2, middle, 0)
 
     def inverse_y(c, carry):
-        arrived(2, c, recv3)
-        y_transform(recv3, send4, c, False)
-        exchange(3, c, send4, recv4, group, in_plane)
+        for h in range(2):
+            n = 3 * h + c
+            arrived(3 + h, c, n, recv3)
+            re, im = recv3[n, :, 0], recv3[n, :, 1]
+            rhs[0, :, h, :, 0:128] = re
+            rhs[0, :, h, :, 128:256] = im
+            rhs[1, :, h, :, 0:128] = -im
+            rhs[1, :, h, :, 128:256] = re
+        for m in range(2):
+            out = jnp.dot(
+                ty[256 * m:256 * m + 256, :], rhs[...].reshape(1024, 256), preferred_element_type=F32
+            )
+            out = out.astype(BF16).reshape(8, 32, 256)
+            send4[c, 8 * m:8 * m + 8, 0] = out[:, :, 0:128]
+            send4[c, 8 * m:8 * m + 8, 1] = out[:, :, 128:256]
+        exchange(5, c, c, send4, recv4, group, in_plane)
         return carry
 
     lax.fori_loop(0, 3, inverse_y, 0)
@@ -265,13 +286,13 @@
         )
 
     def inverse_z(c, carry):
-        arrived(3, c, recv4)
+        arrived(5, c, c, recv4)
         for ro in range(2):
             for y in (0, 16):
-                parts = [recv4[c, s, ro, y:y + 16, :].astype(F32) for s in range(16)]
+                parts = [recv4[c, s, ro, y:y + 16, :] for s in range(16)]
                 parts = swap_index_and_lanes(parts, 8)
                 for x in range(16):
-                    zin[x, y:y + 16, 128 * ro:128 * ro + 128] = parts[x].astype(BF16)
+                    zin[x, y:y + 16, 128 * ro:128 * ro + 128] = parts[x]
         for h in range(2):
             rows = slice(8 * h, 8 * h + 8)
             out = jnp.dot(zin[rows].reshape(256, 256), iz[...], preferred_element_type=F32)
@@ -295,10 +316,11 @@
     transport(vel_ref, out_ref, halo)
 
     def finish(c, carry):
-        sent(0, c, send1)
-        sent(1, c, send2)
-        sent(2, c, send3)
-        sent(3, c, send4)
+        sent(0, c, c, send1)
+        for h in range(2):
+            sent(1 + h, c, 3 * h + c, send2)
+            sent(3 + h, c, 3 * h + c, send3)
+        sent(5, c, c, send4)
         to_partner(c).wait_send()
         return carry
 
@@ -349,20 +371,24 @@
             copies[4].start()
         slot = lax.broadcasted_iota(jnp.int32, (16, 128), 1) // 4
         for tile in range(first, first + count):
-            packed = jnp.zeros((16, 128), F32)
+            edges = [None] * 32
             for t in range(2):
                 for i, x in enumerate(TILES[tile]):
                     slab = 4 * t + i
                     self.stage[0, 2 * slab:2 * slab + 2, :] = state[step, t, 2 + x, 70:72, :]
                     self.stage[1, 2 * slab:2 * slab + 2, :] = state[step, t, 2 + x, 8:10, :]
                     for b in range(4):
-                        edge = pltpu.roll(
-                            state[step, t, 2 + x, 8 + 16 * b:24 + 16 * b, :], (2 + 32 * b + 4 * slab) % 128, 1
+                        edges[8 * b + slab] = pltpu.roll(
+                            state[step, t, 2 + x, 8 + 16 * b:24 + 16 * b, :].astype(BF16),
+                            (2 + 32 * b + 4 * slab) % 128, 1,
                         )
-                        packed = jnp.where(slot == 8 * b + slab, edge, packed)
             self.ysend[step, 0, tile] = self.stage[0].astype(BF16)
             self.ysend[step, 1, tile] = self.stage[1].astype(BF16)
-            self.zsend[step, tile] = packed.astype(BF16)
+            bit = 1
+            while len(edges) > 1:
+                edges = [jnp.where((slot & bit) != 0, edges[n + 1], edges[n]) for n in range(0, len(edges), 2)]
+                bit *= 2
+            self.zsend[step, tile] = edges[0]
         for copy in copies[:3]:
             copy.start()
 
@@ -377,7 +403,7 @@
         for tile in range(first, first + count):
             self.stage[0] = self.yrecv[step, 0, tile].astype(F32)
             self.stage[1] = self.yrecv[step, 1, tile].astype(F32)
-            packed = self.zrecv[step, tile].astype(F32)
+            packed = self.zrecv[step, tile]
             for t in range(2):
                 for i, x in enumerate(TILES[tile]):
                     slab = 4 * t + i
@@ -386,7 +412,7 @@
                     for b in range(4):
                         self.ends[t, x, 16 * b:16 * b + 16, :] = pltpu.roll(
                             packed, (254 - 32 * b - 4 * slab) % 128, 1
-                        )
+                        ).astype(F32)
 
 
 def transport(vel, out_ref, halo):
@@ -466,6 +492,7 @@
     any_spec = pl.BlockSpec(memory_space=pl.ANY)
     vmem = pl.BlockSpec(memory_space=pltpu.VMEM)
     slab = (3, 16, 2, 32, 128)
+    half_slab = (6, 16, 2, 16, 128)
     dma = pltpu.SemaphoreType.DMA
     return pl.pallas_call(
         fused_kernel,
@@ -484,13 +511,15 @@
             pltpu.VMEM((512, 512), BF16),
             pltpu.VMEM((512, 512), BF16),
             pltpu.VMEM((16, 32, 256), F32),
-            pltpu.VMEM((1024, 256), BF16),
-            pltpu.VMEM((8, 32, 512), BF16),
-            pltpu.VMEM((3, 256, 512), F32),
-            pltpu.VMEM((3, 256, 512), BF16),
+            pltpu.VMEM((2, 16, 2, 16, 256), BF16),
+            pltpu.VMEM((3, 8, 16, 512), BF16),
+            pltpu.VMEM((3, 8, 16, 512), F32),
+            pltpu.VMEM((3, 8, 16, 512), BF16),
             pltpu.VMEM((16, 32, 256), BF16),
         ]
-        + [pltpu.VMEM(slab, BF16)] * 8
+        + [pltpu.VMEM(slab, BF16)] * 2
+        + [pltpu.VMEM(half_slab, BF16)] * 4
+        + [pltpu.VMEM(slab, BF16)] * 2
         + [pltpu.VMEM((3, 16, 32, 128), BF16)] * 2
         + [
             pltpu.VMEM((2, 64, 128), jnp.int32),
@@ -501,7 +530,7 @@
         + [pltpu.VMEM((STEPS, 2, 2, 2, 64, 128), BF16)] * 2
         + [pltpu.VMEM((STEPS, 2, 4, 16, 128), BF16)] * 2
         + [pltpu.VMEM((STEPS, 4, 16, 128), BF16)] * 2
-        + [dma((9,)), dma((4, 3)), dma((4, 3)), dma((3,)), dma((3,))]
+        + [dma((9,)), dma((6, 3)), dma((6, 3)), dma((3,)), dma((3,))]
         + [dma((STEPS, 2)), dma((STEPS, 2)), dma((STEPS, 3, 3)), dma((STEPS, 3, 3))],
         compiler_params=pltpu.CompilerParams(
             collective_id=0, has_side_effects=True, vmem_limit_bytes=VMEM_LIMIT

time: 99.1 us -> 97.8 us (0.987); the launches traced: 98.9 us -> 96.6 us
  Pallas kernels: 94.5 us -> 92.1 us
    pallas_call x1, Pallas kernels: 94.5 us -> 92.1 us  [fused(): pl.pallas_call(fused_kernel, out_shape=(jax.ShapeDtypeStruct((3, 16, 64,...]
where the time goes in v3:
time: 97.8 us; the launch traced here: 96.6 us
  Pallas kernels  92.1 us (94%)
  local copies, waits for them, and re-layouts  3.79 us (4%)
    pallas_call x1, Pallas kernels, fused(): pl.pallas_call(fused_kernel, out_shape=(jax.ShapeDtypeStruct((3, 16, 64,...  92.1 us
    unnamed x4, local copies, waits for them, and re-layouts  3.79 us

profile of v3, /device:TPU:24, one launch (start us, length us, event | category | flops | bytes accessed | tf_op | source)
XLA Modules:
  0.0 96.6 jit_solution(13509920758153081206)
XLA Ops:
  0.6 92.1 %stokes_transport.1 = (f32[3,16,64,128]{3,2,1,0:T(8,128)}, f32[2,16,64,128]{3,2,1,0:T(8,128)}) custom-call(bf16[3,16,32,256]{3,2,1,0:T(8,128)(2,1)} %force_hbm.1, s32[16,32,256]{2,1,0:T(8,128)} %mask_hbm.1, f32[2,16,64,128]{3,2,1,0:T(8,128)} %tracers_hbm.1, s32[2,64,128]{2,1,0:T(8,128)} %inlet_hbm.1, bf16[256,256]{1,0:T(8,128)(2,1)} %constant.10.clone.fz_hbm, ...), custom_call_target="tpu_custom_call" | custom-call | tf_op jit(solution)/shard_map/stokes_transport/pallas_call | solution.py:497
  92.8 0.0 copy-start
  92.8 2.8 %copy.13 = f32[3,16,64,128]{3,2,1,0:T(8,128)} copy(f32[3,16,64,128]{3,2,1,0:T(8,128)} %get-tuple-element.4) | data formatting | bytes 3145728
  95.6 0.0 copy-done
  95.6 1.0 %copy.14 = f32[2,16,64,128]{3,2,1,0:T(8,128)} copy(f32[2,16,64,128]{3,2,1,0:T(8,128)S(1)} %copy-done) | data formatting | bytes 2097152
Async XLA Ops:
  92.8 2.8 %copy-start = (f32[2,16,64,128]{3,2,1,0:T(8,128)S(1)}, f32[2,16,64,128]{3,2,1,0:T(8,128)}, u32[]{:S(2)}) copy-start(f32[2,16,64,128]{3,2,1,0:T(8,128)} %get-tuple-element.5) | copy-start | bytes 3145732

commit v4 on v3

--- a/solution.py
+++ b/solution.py
@@ -77,7 +77,7 @@
 
 
 TILES = ((0, 1, 14, 15), (2, 3, 4, 5), (6, 7, 8, 9), (10, 11, 12, 13))
-GROUPS = ((0, 1), (1, 1), (2, 2))
+GROUPS = ((0, 1), (1, 1), (2, 1), (3, 1))
 
 
 def fused_kernel(
@@ -125,7 +125,8 @@
             ).start()
             return carry
 
-        lax.fori_loop(1, 16, one, 0)
+        for k in range(1, 16):
+            one(k, 0)
         pltpu.make_async_copy(send.at[n, me], recv.at[n, me], recv_sem.at[row, c]).start()
 
     def arrived(row, c, n, recv):
@@ -194,7 +195,7 @@
     for t in range(2):
         plane = state[0, t, 2, 8:72, :]
         state[0, t, 2, 8:72, :] = jnp.where(gx == 0, jnp.where(inlet[t] == 1, 1.0, plane), plane)
-    for group_id in range(3):
+    for group_id in range(len(GROUPS)):
         halo.send(0, group_id)
 
     loads[4].wait()
@@ -463,7 +464,7 @@
         lax.fori_loop(0, 4 * count, plane, 0)
 
     def advance(step, last):
-        for group_id in range(3):
+        for group_id in range(len(GROUPS)):
             halo.receive(step, group_id)
             compute(step, group_id, last)
             if not last:
@@ -477,7 +478,7 @@
     advance(STEPS - 1, True)
 
     def finish(step, carry):
-        for group_id in range(3):
+        for group_id in range(len(GROUPS)):
             for copy in halo.copies(step, group_id):
                 copy.wait_send()
         return carry
@@ -497,8 +498,8 @@
     return pl.pallas_call(
         fused_kernel,
         out_shape=(
-            jax.ShapeDtypeStruct((3, 16, 64, 128), F32),
-            jax.ShapeDtypeStruct((2, 16, 64, 128), F32),
+            pltpu.VMEM((3, 16, 64, 128), F32),
+            pltpu.VMEM((2, 16, 64, 128), F32),
         ),
         in_specs=[any_spec] * 9,
         out_specs=(vmem, vmem),
@@ -531,7 +532,7 @@
         + [pltpu.VMEM((STEPS, 2, 4, 16, 128), BF16)] * 2
         + [pltpu.VMEM((STEPS, 4, 16, 128), BF16)] * 2
         + [dma((9,)), dma((6, 3)), dma((6, 3)), dma((3,)), dma((3,))]
-        + [dma((STEPS, 2)), dma((STEPS, 2)), dma((STEPS, 3, 3)), dma((STEPS, 3, 3))],
+        + [dma((STEPS, 2)), dma((STEPS, 2)), dma((STEPS, len(GROUPS), 3)), dma((STEPS, len(GROUPS), 3))],
         compiler_params=pltpu.CompilerParams(
             collective_id=0, has_side_effects=True, vmem_limit_bytes=VMEM_LIMIT
         ),

time: 97.8 us -> 92.8 us (0.949)
  Pallas kernels: 92.1 us -> 89.1 us
  local copies, waits for them, and re-layouts: 3.79 us -> 2.11 us
    pallas_call x1, Pallas kernels: 92.1 us -> 89.1 us  [fused(): pl.pallas_call(fused_kernel, out_shape=(pltpu.VMEM((3, 16, 64, 128), F32)...]
    unnamed x4 -> x2, local copies, waits for them, and re-layouts: 3.79 us -> 2.11 us
where the time goes in v4:
time: 92.8 us; the launch traced here: 91.8 us
  Pallas kernels  89.1 us (96%)
  local copies, waits for them, and re-layouts  2.11 us (2%)
    pallas_call x1, Pallas kernels, fused(): pl.pallas_call(fused_kernel, out_shape=(pltpu.VMEM((3, 16, 64, 128), F32)...  89.1 us
    unnamed x2, local copies, waits for them, and re-layouts  2.11 us

profile of v4, /device:TPU:24, one launch (start us, length us, event | category | flops | bytes accessed | tf_op | source)
XLA Modules:
  0.0 91.8 jit_solution(6398241077778700784)
XLA Ops:
  0.6 89.1 %stokes_transport.1 = (f32[3,16,64,128]{3,2,1,0:T(8,128)S(1)}, f32[2,16,64,128]{3,2,1,0:T(8,128)S(1)}) custom-call(bf16[3,16,32,256]{3,2,1,0:T(8,128)(2,1)} %force_hbm.1, s32[16,32,256]{2,1,0:T(8,128)} %mask_hbm.1, f32[2,16,64,128]{3,2,1,0:T(8,128)} %tracers_hbm.1, s32[2,64,128]{2,1,0:T(8,128)} %inlet_hbm.1, bf16[256,256]{1,0:T(8,128)(2,1)} %constant.10.clone.fz_hbm, ...), custom_call_target="tpu_custom_call" | custom-call | tf_op jit(solution)/shard_map/stokes_transport/pallas_call | solution.py:498
  89.7 1.1 %copy.13 = f32[3,16,64,128]{3,2,1,0:T(8,128)} copy(f32[3,16,64,128]{3,2,1,0:T(8,128)S(1)} %get-tuple-element.2) | data formatting | bytes 3145728
  90.9 1.0 %copy.14 = f32[2,16,64,128]{3,2,1,0:T(8,128)} copy(f32[2,16,64,128]{3,2,1,0:T(8,128)S(1)} %get-tuple-element.3) | data formatting | bytes 2097152

commit v5 on v4

--- a/solution.py
+++ b/solution.py
@@ -96,6 +96,15 @@
     def in_column(to):
         return (to, gy, gz)
 
+    barrier = pltpu.get_barrier_semaphore()
+
+    def greet(k, carry):
+        pl.semaphore_signal(barrier, inc=1, device_id=in_plane((group + k) % 16), device_id_type=MESH)
+        pl.semaphore_signal(barrier, inc=1, device_id=in_column((gx + k) % 16), device_id_type=MESH)
+        return carry
+
+    lax.fori_loop(1, 16, greet, 0)
+
     loads = [
         pltpu.make_async_copy(src, dst, load_sem.at[n])
         for n, (src, dst) in enumerate(
@@ -105,15 +114,6 @@
     ]
     for load in loads:
         load.start()
-
-    barrier = pltpu.get_barrier_semaphore()
-
-    def greet(k, carry):
-        pl.semaphore_signal(barrier, inc=1, device_id=in_plane((group + k) % 16), device_id_type=MESH)
-        pl.semaphore_signal(barrier, inc=1, device_id=in_column((gx + k) % 16), device_id_type=MESH)
-        return carry
-
-    lax.fori_loop(1, 16, greet, 0)
 
     def exchange(row, c, n, send, recv, me, place):
         def one(k, carry):
@@ -247,7 +247,15 @@
                     parts = swap_index_and_lanes(parts, 1)
                     for i in range(8):
                         send3[n, 8 * hi + i, ro] = parts[i]
-            exchange(3 + h, c, n, send3, recv3, gx, in_column)
+
+            @pl.when((h == 1) & (c > 0))
+            def _():
+                exchange(3, c, c, send3, recv3, gx, in_column)
+
+            @pl.when((h == 1) | (c == 0))
+            def _():
+                exchange(3 + h, c, n, send3, recv3, gx, in_column)
+
             return carry
 
         lax.fori_loop(0, 3, inverse_x, 0)
@@ -365,6 +373,16 @@
         state = self.state
         first, count = GROUPS[group_id]
         copies = self.copies(step, group_id)
+        for tile in range(first, first + count):
+            for t in range(2):
+                for i, x in enumerate(TILES[tile]):
+                    slab = 4 * t + i
+                    self.stage[0, 2 * slab:2 * slab + 2, :] = state[step, t, 2 + x, 70:72, :]
+                    self.stage[1, 2 * slab:2 * slab + 2, :] = state[step, t, 2 + x, 8:10, :]
+            self.ysend[step, 0, tile] = self.stage[0].astype(BF16)
+            self.ysend[step, 1, tile] = self.stage[1].astype(BF16)
+        copies[0].start()
+        copies[1].start()
         if group_id == 0:
             self.xsend[step, 0] = state[step, :, 16:18, 8:72, :].astype(BF16)
             self.xsend[step, 1] = state[step, :, 2:4, 8:72, :].astype(BF16)
@@ -376,22 +394,17 @@
             for t in range(2):
                 for i, x in enumerate(TILES[tile]):
                     slab = 4 * t + i
-                    self.stage[0, 2 * slab:2 * slab + 2, :] = state[step, t, 2 + x, 70:72, :]
-                    self.stage[1, 2 * slab:2 * slab + 2, :] = state[step, t, 2 + x, 8:10, :]
                     for b in range(4):
                         edges[8 * b + slab] = pltpu.roll(
                             state[step, t, 2 + x, 8 + 16 * b:24 + 16 * b, :].astype(BF16),
                             (2 + 32 * b + 4 * slab) % 128, 1,
                         )
-            self.ysend[step, 0, tile] = self.stage[0].astype(BF16)
-            self.ysend[step, 1, tile] = self.stage[1].astype(BF16)
             bit = 1
             while len(edges) > 1:
                 edges = [jnp.where((slot & bit) != 0, edges[n + 1], edges[n]) for n in range(0, len(edges), 2)]
                 bit *= 2
             self.zsend[step, tile] = edges[0]
-        for copy in copies[:3]:
-            copy.start()
+        copies[2].start()
 
     def receive(self, step, group_id):
         state = self.state

time: 92.8 us -> 92.1 us (level)
  no operation moved by 1% of the time
where the time goes in v5:
time: 92.1 us; the launch traced here: 91.1 us
  Pallas kernels  88.4 us (96%)
  local copies, waits for them, and re-layouts  2.11 us (2%)
    pallas_call x1, Pallas kernels, fused(): pl.pallas_call(fused_kernel, out_shape=(pltpu.VMEM((3, 16, 64, 128), F32)...  88.4 us
    unnamed x2, local copies, waits for them, and re-layouts  2.11 us

profile of v5, /device:TPU:24, one launch (start us, length us, event | category | flops | bytes accessed | tf_op | source)
XLA Modules:
  0.0 91.1 jit_solution(8649631970534589614)
XLA Ops:
  0.6 88.4 %stokes_transport.1 = (f32[3,16,64,128]{3,2,1,0:T(8,128)S(1)}, f32[2,16,64,128]{3,2,1,0:T(8,128)S(1)}) custom-call(bf16[3,16,32,256]{3,2,1,0:T(8,128)(2,1)} %force_hbm.1, s32[16,32,256]{2,1,0:T(8,128)} %mask_hbm.1, f32[2,16,64,128]{3,2,1,0:T(8,128)} %tracers_hbm.1, s32[2,64,128]{2,1,0:T(8,128)} %inlet_hbm.1, bf16[256,256]{1,0:T(8,128)(2,1)} %constant.10.clone.fz_hbm, ...), custom_call_target="tpu_custom_call" | custom-call | tf_op jit(solution)/shard_map/stokes_transport/pallas_call | solution.py:511
  89.0 1.1 %copy.13 = f32[3,16,64,128]{3,2,1,0:T(8,128)} copy(f32[3,16,64,128]{3,2,1,0:T(8,128)S(1)} %get-tuple-element.2) | data formatting | bytes 3145728
  90.1 1.0 %copy.14 = f32[2,16,64,128]{3,2,1,0:T(8,128)} copy(f32[2,16,64,128]{3,2,1,0:T(8,128)S(1)} %get-tuple-element.3) | data formatting | bytes 2097152

commit v6 on v5

--- a/solution.py
+++ b/solution.py
@@ -288,9 +288,11 @@
     own = pl.multiple_of(gz * 32, 32)
     other = pl.multiple_of((1 - gz) * 32, 32)
 
-    def to_partner(c):
+    def to_partner(c, h):
+        planes = pl.ds(8 * h, 8)
         return pltpu.make_async_remote_copy(
-            src_ref=sendv.at[c], dst_ref=recvv.at[c], send_sem=vsend_sem.at[c], recv_sem=vrecv_sem.at[c],
+            src_ref=sendv.at[c, planes], dst_ref=recvv.at[c, planes],
+            send_sem=vsend_sem.at[c, h], recv_sem=vrecv_sem.at[c, h],
             device_id=(gx, gy, 1 - gz), device_id_type=MESH,
         )
 
@@ -302,22 +304,24 @@
                 parts = swap_index_and_lanes(parts, 8)
                 for x in range(16):
                     zin[x, y:y + 16, 128 * ro:128 * ro + 128] = parts[x]
+        mine = pl.ds(pl.multiple_of(gz * 128, 128), 128)
+        theirs = pl.ds(pl.multiple_of((1 - gz) * 128, 128), 128)
         for h in range(2):
             rows = slice(8 * h, 8 * h + 8)
             out = jnp.dot(zin[rows].reshape(256, 256), iz[...], preferred_element_type=F32)
             zbuf[rows] = out.reshape(8, 32, 256)
-        mine = pl.ds(pl.multiple_of(gz * 128, 128), 128)
-        theirs = pl.ds(pl.multiple_of((1 - gz) * 128, 128), 128)
-        sendv[c] = zbuf[:, :, theirs].astype(BF16)
-        to_partner(c).start()
+            sendv[c, rows] = zbuf[rows, :, theirs].astype(BF16)
+            to_partner(c, h).start()
         vel_ref[c, :, pl.ds(own, 32), :] = zbuf[:, :, mine]
         return carry
 
     lax.fori_loop(0, 3, inverse_z, 0)
 
     def gather(c, carry):
-        to_partner(c).wait_recv()
-        vel_ref[c, :, pl.ds(other, 32), :] = recvv[c].astype(F32)
+        for h in range(2):
+            to_partner(c, h).wait_recv()
+            rows = slice(8 * h, 8 * h + 8)
+            vel_ref[c, rows, pl.ds(other, 32), :] = recvv[c, rows].astype(F32)
         return carry
 
     lax.fori_loop(0, 3, gather, 0)
@@ -330,7 +334,8 @@
             sent(1 + h, c, 3 * h + c, send2)
             sent(3 + h, c, 3 * h + c, send3)
         sent(5, c, c, send4)
-        to_partner(c).wait_send()
+        for h in range(2):
+            to_partner(c, h).wait_send()
         return carry
 
     lax.fori_loop(0, 3, finish, 0)
@@ -544,7 +549,7 @@
         + [pltpu.VMEM((STEPS, 2, 2, 2, 64, 128), BF16)] * 2
         + [pltpu.VMEM((STEPS, 2, 4, 16, 128), BF16)] * 2
         + [pltpu.VMEM((STEPS, 4, 16, 128), BF16)] * 2
-        + [dma((9,)), dma((6, 3)), dma((6, 3)), dma((3,)), dma((3,))]
+        + [dma((9,)), dma((6, 3)), dma((6, 3)), dma((3, 2)), dma((3, 2))]
         + [dma((STEPS, 2)), dma((STEPS, 2)), dma((STEPS, len(GROUPS), 3)), dma((STEPS, len(GROUPS), 3))],
         compiler_params=pltpu.CompilerParams(
             collective_id=0, has_side_effects=True, vmem_limit_bytes=VMEM_LIMIT

time: 92.1 us -> 92.1 us (level)
  no operation moved by 1% of the time
where the time goes in v6:
time: 92.1 us; the launch traced here: 91.2 us
  Pallas kernels  88.4 us (96%)
  local copies, waits for them, and re-layouts  2.11 us (2%)
    pallas_call x1, Pallas kernels, fused(): pl.pallas_call(fused_kernel, out_shape=(pltpu.VMEM((3, 16, 64, 128), F32)...  88.4 us
    unnamed x2, local copies, waits for them, and re-layouts  2.11 us

profile of v6, /device:TPU:24, one launch (start us, length us, event | category | flops | bytes accessed | tf_op | source)
XLA Modules:
  0.0 91.2 jit_solution(14558036263315358141)
XLA Ops:
  0.6 88.4 %stokes_transport.1 = (f32[3,16,64,128]{3,2,1,0:T(8,128)S(1)}, f32[2,16,64,128]{3,2,1,0:T(8,128)S(1)}) custom-call(bf16[3,16,32,256]{3,2,1,0:T(8,128)(2,1)} %force_hbm.1, s32[16,32,256]{2,1,0:T(8,128)} %mask_hbm.1, f32[2,16,64,128]{3,2,1,0:T(8,128)} %tracers_hbm.1, s32[2,64,128]{2,1,0:T(8,128)} %inlet_hbm.1, bf16[256,256]{1,0:T(8,128)(2,1)} %constant.10.clone.fz_hbm, ...), custom_call_target="tpu_custom_call" | custom-call | tf_op jit(solution)/shard_map/stokes_transport/pallas_call | solution.py:516
  89.0 1.1 %copy.13 = f32[3,16,64,128]{3,2,1,0:T(8,128)} copy(f32[3,16,64,128]{3,2,1,0:T(8,128)S(1)} %get-tuple-element.2) | data formatting | bytes 3145728
  90.2 1.0 %copy.14 = f32[2,16,64,128]{3,2,1,0:T(8,128)} copy(f32[2,16,64,128]{3,2,1,0:T(8,128)S(1)} %get-tuple-element.3) | data formatting | bytes 2097152
